TPU v7x, 32 devices: a whole 2x2x4 slice. The times are simulated.
32 devices in a mesh: groups: 2 (over y), row: 4 (over z), col: 4 (over x, core).
Axes of the slice: x: 2, y: 2, z: 4, core: 2. Of those that a mesh axis runs over, the one named last changes fastest.
Arguments:
- alignment: bfloat16 [256, 128, 256], P(('groups', 'row'), 'col'), parts along dimension 0, may hold values from -6 to 6
- sequence_mask: int32 [256], P('groups'), parts along dimension 0, may hold values 0 or 1
- residue_mask: int32 [256], P('groups'), parts along dimension 0, may hold values 0 or 1
- layer_norm_gain: float32 [256], replicated, may hold values from 0.5 to 1.5
- norm_shift: float32 [256], replicated, may hold values from -3 to 3
- proj_weight: bfloat16 [256, 64], replicated, may hold values from -0.375 to 0.375
- proj_bias: float32 [64], replicated, may hold values from -3 to 3
- out_weight: bfloat16 [1024, 128], replicated, may hold values from -2 to 2
- out_bias: float32 [128], replicated, may hold values from -4 to 4
- cotangent: bfloat16 [256, 128, 128], P(('groups', 'row'), 'col'), parts along dimension 0, may hold values from -2 to 2
Outputs:
- pair_output_update: bfloat16 [256, 128, 128], P(('groups', 'row'), 'col'), parts along dimension 0
- alignment_gradient: bfloat16 [256, 128, 256], P(('groups', 'row'), 'col'), parts along dimension 0
- norm_gain_gradient: float32 [512], P('groups'), parts along dimension 0
- norm_shift_gradient: float32 [512], P('groups'), parts along dimension 0
- projection_weight_gradient: float32 [512, 64], P('groups'), parts along dimension 0
- projection_bias_gradient: float32 [128], P('groups'), parts along dimension 0
- output_weight_gradient: float32 [2048, 128], P('groups'), parts along dimension 0
There are 2 independent parts, one for each index of `groups`. A program takes and returns all parts, laid end to end along the dimension named above; an argument that names none is the same for every part. Nothing has to cross between parts.
All inputs are finite; a program needn't handle non-finite values.
Results may differ from a plain program's by a relative error of at most 0.0074.
Values may be sent and summed in bfloat16 or wider, within the bound.
A program may use at most 64 MiB of HBM per device.

v0:
```python
import functools

import jax
import jax.numpy as jnp
from jax import lax
from jax.experimental import pallas as pl
from jax.experimental.pallas import tpu as pltpu
from jax.sharding import PartitionSpec as P

EPSILON = 1e-05
LANES = 128
MESH = pl.DeviceIdType.MESH


def normalize(values, layer_norm_gain, norm_shift):
    widened = values.astype(jnp.float32)
    centred = widened - jnp.mean(widened, axis=-1, keepdims=True)
    inverse_deviation = lax.rsqrt(jnp.mean(centred * centred, axis=-1, keepdims=True) + EPSILON)
    scaled_product = centred * inverse_deviation
    return (
        scaled_product,
        inverse_deviation,
        (scaled_product * layer_norm_gain + norm_shift).astype(jnp.bfloat16),
    )


def layer_norm_backward_pass(
    normalized_input_gradient, scaled_product, inverse_deviation, layer_norm_gain
):
    grad_scaled = normalized_input_gradient * layer_norm_gain
    first = jnp.mean(grad_scaled, axis=-1, keepdims=True)
    second = jnp.mean(grad_scaled * scaled_product, axis=-1, keepdims=True)
    return inverse_deviation * (grad_scaled - first - scaled_product * second)


def route_gather_row(rows, cols):
    return dict(
        sends=rows,
        slots=rows,
        send=lambda t, r, c: (None, lax.rem(r + t, rows), c),
        mine=lambda r, c: r,
        source=lambda s, r, c: (s, c),
    )


def route_scatter_row(rows, cols):
    return dict(
        sends=rows,
        slots=rows,
        send=lambda t, r, c: (lax.rem(r + t, rows), lax.rem(r + t, rows), c),
        mine=lambda r, c: r,
        source=lambda s, r, c: (s, c),
    )


def route_gather_col(rows, cols):
    return dict(
        sends=cols,
        slots=cols,
        send=lambda t, r, c: (None, r, lax.rem(c + t, cols)),
        mine=lambda r, c: c,
        source=lambda s, r, c: (r, s),
    )


def route_scatter_col(rows, cols):
    return dict(
        sends=cols,
        slots=cols,
        send=lambda t, r, c: (lax.rem(c + t, cols), r, lax.rem(c + t, cols)),
        mine=lambda r, c: c,
        source=lambda s, r, c: (r, s),
    )


def route_tiles(rows, cols):
    factor = cols // rows
    return dict(
        sends=cols,
        slots=rows * factor,
        send=lambda t, r, c: (None, c // factor, lax.rem(c + t, cols)),
        mine=lambda r, c: r * factor + lax.rem(c, factor),
        source=lambda s, r, c: (s // factor, r * factor + lax.rem(s, factor)),
    )


def route_untile(rows, cols):
    factor = cols // rows

    def send(t, r, c):
        piece = lax.rem(r * factor + t, rows * factor)
        return piece, piece // factor, r * factor + lax.rem(piece, factor)

    return dict(
        sends=rows * factor,
        slots=cols,
        send=send,
        mine=lambda r, c: c,
        source=lambda s, r, c: (c // factor, s),
    )


def route_scatter_all(rows, cols):
    count = rows * cols

    def send(t, r, c):
        goal = lax.rem(r * cols + c + t, count)
        return goal, goal // cols, lax.rem(goal, cols)

    return dict(
        sends=count,
        slots=count,
        send=send,
        mine=lambda r, c: r * cols + c,
        source=lambda s, r, c: (s // cols, lax.rem(s, cols)),
    )


def route_gather_all(rows, cols):
    route = route_scatter_all(rows, cols)
    scatter_send = route["send"]
    route["send"] = lambda t, r, c: (None,) + scatter_send(t, r, c)[1:]
    return route


def exchange_kernel(routes, rows, cols, along_row, *refs):
    count = len(routes)
    sources, outs = refs[:count], refs[count : 2 * count]
    send_sems = refs[2 * count : 3 * count]
    recv_sems = refs[3 * count : 4 * count]
    local_sems = refs[4 * count]
    r = lax.axis_index("row")
    c = lax.axis_index("col")
    total = rows if along_row else rows * cols
    barrier = pltpu.get_barrier_semaphore()

    def greet(t, carry):
        if along_row:
            orow, ocol = lax.rem(r + t, total), c
        else:
            other = lax.rem(r * cols + c + t, total)
            orow, ocol = other // cols, lax.rem(other, cols)
        pl.semaphore_signal(
            barrier,
            inc=1,
            device_id={"row": orow, "col": ocol},
            device_id_type=MESH,
        )
        return carry

    lax.fori_loop(1, total, greet, 0)
    pl.semaphore_wait(barrier, total - 1)

    def describe(k, t):
        piece, trow, tcol = routes[k]["send"](t, r, c)
        source = sources[k] if piece is None else sources[k].at[piece]
        slot = routes[k]["mine"](r, c)
        remote = pltpu.make_async_remote_copy(
            src_ref=source,
            dst_ref=outs[k].at[slot],
            send_sem=send_sems[k].at[t],
            recv_sem=recv_sems[k].at[slot],
            device_id={"row": trow, "col": tcol},
            device_id_type=MESH,
        )
        here = jnp.logical_and(trow == r, tcol == c)
        return remote, source, outs[k].at[slot], here

    for k in range(count):

        def begin(t, carry, k=k):
            remote, source, target, here = describe(k, t)

            @pl.when(here)
            def _():
                local = pltpu.make_async_copy(source, target, local_sems.at[k])
                local.start()
                local.wait()

            @pl.when(jnp.logical_not(here))
            def _():
                remote.start()

            return carry

        lax.fori_loop(0, routes[k]["sends"], begin, 0)

    for k in range(count):

        def finish(t, carry, k=k):
            remote, _, _, here = describe(k, t)

            @pl.when(jnp.logical_not(here))
            def _():
                remote.wait_send()

            return carry

        def receive(s, carry, k=k):
            srow, scol = routes[k]["source"](s, r, c)
            here = jnp.logical_and(srow == r, scol == c)
            arrival = pltpu.make_async_remote_copy(
                src_ref=outs[k].at[s],
                dst_ref=outs[k].at[s],
                send_sem=send_sems[k].at[0],
                recv_sem=recv_sems[k].at[s],
                device_id={"row": srow, "col": scol},
                device_id_type=MESH,
            )

            @pl.when(jnp.logical_not(here))
            def _():
                arrival.wait_recv()

            return carry

        lax.fori_loop(0, routes[k]["slots"], receive, 0)
        lax.fori_loop(0, routes[k]["sends"], finish, 0)


def exchange(arrays, makers, rows, cols, collective_id, along_row=False):
    routes = [maker(rows, cols) for maker in makers]
    shapes = []
    for array, route in zip(arrays, routes):
        block = array.shape if route["send"](0, 0, 0)[0] is None else array.shape[1:]
        shapes.append(jax.ShapeDtypeStruct((route["slots"],) + block, array.dtype))
    return pl.pallas_call(
        functools.partial(exchange_kernel, routes, rows, cols, along_row),
        out_shape=shapes,
        in_specs=[pl.BlockSpec(memory_space=pltpu.VMEM)] * len(arrays),
        out_specs=[pl.BlockSpec(memory_space=pltpu.VMEM)] * len(arrays),
        scratch_shapes=[pltpu.SemaphoreType.DMA((route["sends"],)) for route in routes]
        + [pltpu.SemaphoreType.DMA((route["slots"],)) for route in routes]
        + [pltpu.SemaphoreType.DMA((len(routes),))],
        compiler_params=pltpu.CompilerParams(collective_id=collective_id, has_side_effects=True),
    )(*arrays)


def pair_kernel(
    res,
    hidden,
    lt_ref,
    l_ref,
    r_ref,
    w_ref,
    cot_ref,
    div_ref,
    bias_ref,
    pair_ref,
    gw_ref,
    gl_ref,
    gr_ref,
    pre_ref,
    gpre_ref,
    glacc_ref,
):
    step = pl.program_id(0)
    fold = LANES // res
    seqs = r_ref.shape[0]
    major = l_ref.shape[0] // hidden

    @pl.when(step == 0)
    def _():
        gpre_ref[...] = (cot_ref[...].astype(jnp.float32) / div_ref[...]).astype(jnp.bfloat16)
        pre_ref[...] = jnp.zeros_like(pre_ref)
        glacc_ref[...] = jnp.zeros_like(glacc_ref)

    group = lax.broadcasted_iota(jnp.int32, (seqs, LANES), 1) // res
    wide = jnp.concatenate([group] * fold, axis=1)

    def spread(x):
        out = x
        for k in range(1, fold):
            out = out + pltpu.roll(x, k * res, 1)
        return out

    chunk = r_ref[...].astype(jnp.float32)
    copies = jnp.concatenate(
        [spread(jnp.where(group == d, chunk, 0.0)) for d in range(fold)], axis=1
    )
    masked = jnp.concatenate(
        [jnp.where(wide == i, copies, 0.0).astype(jnp.bfloat16) for i in range(fold)], axis=0
    )
    tile = jnp.dot(l_ref[...], masked, preferred_element_type=jnp.float32).astype(jnp.bfloat16)
    products = jnp.concatenate(
        [
            jnp.concatenate(
                [
                    tile[i * hidden : (i + 1) * hidden, d * LANES : (d + 1) * LANES]
                    for i in range(major)
                ],
                axis=1,
            )
            for d in range(fold)
        ],
        axis=0,
    )
    weight = w_ref[...]
    grad_pre = gpre_ref[...]
    pre_ref[...] += lax.dot_general(
        products, weight, (((0,), (0,)), ((), ())), preferred_element_type=jnp.float32
    )
    gw_ref[...] = jnp.dot(products, grad_pre, preferred_element_type=jnp.float32).astype(
        gw_ref.dtype
    )
    grad_products = lax.dot_general(
        weight, grad_pre, (((1,), (1,)), ((), ())), preferred_element_type=jnp.float32
    ).astype(jnp.bfloat16)
    grad_tile = jnp.concatenate(
        [
            jnp.concatenate(
                [
                    grad_products[d * hidden : (d + 1) * hidden, i * LANES : (i + 1) * LANES]
                    for d in range(fold)
                ],
                axis=1,
            )
            for i in range(major)
        ],
        axis=0,
    )
    glacc_ref[...] += lax.dot_general(
        masked, grad_tile, (((1,), (1,)), ((), ())), preferred_element_type=jnp.float32
    )
    grad_right = jnp.zeros((seqs, fold * LANES), jnp.float32)
    for i in range(fold):
        part = jnp.dot(
            lt_ref[i * seqs : (i + 1) * seqs, :], grad_tile, preferred_element_type=jnp.float32
        )
        grad_right = jnp.where(wide == i, part, grad_right)
    packed = jnp.zeros((seqs, LANES), jnp.float32)
    for d in range(fold):
        packed = jnp.where(
            group == d, spread(grad_right[:, d * LANES : (d + 1) * LANES]), packed
        )
    gr_ref[...] = packed.astype(gr_ref.dtype)

    @pl.when(step == pl.num_programs(0) - 1)
    def _():
        pair_ref[...] = ((pre_ref[...] + bias_ref[...]) / div_ref[...]).astype(pair_ref.dtype)
        gl_ref[...] = glacc_ref[...].astype(gl_ref.dtype)


def pair_tile(lt, right, weight, cotangent, divisor, bias, res, hidden):
    fold = LANES // res
    pairs, width = cotangent.shape
    seqs = right.shape[0]
    rows = lt.shape[1]

    def whole(shape):
        return pl.BlockSpec(shape, lambda k: (0,) * len(shape))

    return pl.pallas_call(
        functools.partial(pair_kernel, res, hidden),
        grid=(hidden // fold,),
        in_specs=[
            whole(lt.shape),
            whole(lt.shape[::-1]),
            pl.BlockSpec((seqs, LANES), lambda k: (0, k)),
            pl.BlockSpec((fold * hidden, width), lambda k: (k, 0)),
            whole((pairs, width)),
            whole((pairs, 1)),
            whole((1, width)),
        ],
        out_specs=[
            whole((pairs, width)),
            pl.BlockSpec((fold * hidden, width), lambda k: (k, 0)),
            whole(lt.shape),
            pl.BlockSpec((seqs, LANES), lambda k: (0, k)),
        ],
        out_shape=[
            jax.ShapeDtypeStruct((pairs, width), jnp.bfloat16),
            jax.ShapeDtypeStruct((hidden * hidden, width), jnp.bfloat16),
            jax.ShapeDtypeStruct(lt.shape, jnp.bfloat16),
            jax.ShapeDtypeStruct((seqs, hidden * res), jnp.bfloat16),
        ],
        scratch_shapes=[
            pltpu.VMEM((pairs, width), jnp.float32),
            pltpu.VMEM((pairs, width), jnp.bfloat16),
            pltpu.VMEM((fold * seqs, rows), jnp.float32),
        ],
        compiler_params=pltpu.CompilerParams(dimension_semantics=("arbitrary",)),
    )(lt, lt.T, right, weight, cotangent, divisor, bias)


def shards(
    alignment,
    sequence_mask,
    residue_mask,
    layer_norm_gain,
    norm_shift,
    proj_weight,
    proj_bias,
    out_weight,
    out_bias,
    cotangent,
):
    rows = lax.axis_size("row")
    cols = lax.axis_size("col")
    factor = cols // rows
    row_index = lax.axis_index("row")
    col_index = lax.axis_index("col")
    seq_local, res_local, channels = alignment.shape
    seqs = seq_local * rows
    hidden = proj_weight.shape[1] // 2
    pair_width = out_weight.shape[1]
    tile_rows = res_local * factor
    fold = LANES // res_local
    inner = res_local // fold
    scaled_product, inverse_deviation, normed = normalize(alignment, layer_norm_gain, norm_shift)
    seq_here = lax.dynamic_slice_in_dim(sequence_mask, row_index * seq_local, seq_local)
    res_here = lax.dynamic_slice_in_dim(residue_mask, col_index * res_local, res_local)
    live = (seq_here[:, None] * res_here[None, :]).astype(jnp.float32)
    projected = jnp.dot(
        normed.reshape(-1, channels), proj_weight, preferred_element_type=jnp.float32
    )
    projected = projected.reshape(seq_local, res_local, 2 * hidden) + proj_bias
    masked = (projected * live[:, :, None]).astype(jnp.bfloat16)
    left_send = (
        masked[:, :, :hidden]
        .reshape(seq_local, inner, fold, hidden)
        .transpose(2, 0, 1, 3)
        .reshape(fold, seq_local, inner * hidden)
    )
    right_send = masked[:, :, hidden:].transpose(0, 2, 1).reshape(seq_local, hidden * res_local)
    lefts, rights = exchange(
        [left_send, right_send], [route_tiles, route_gather_row], rows, cols, 0
    )
    lt = (
        lefts.reshape(rows, factor, fold, seq_local, inner * hidden)
        .transpose(2, 0, 3, 1, 4)
        .reshape(fold * seqs, factor * inner * hidden)
    )
    right = rights.reshape(seqs, hidden * res_local)
    kept_count = jnp.sum(sequence_mask).astype(jnp.float32)
    tile_live = lax.dynamic_slice_in_dim(residue_mask, row_index * tile_rows, tile_rows).astype(
        jnp.float32
    )
    column_live = res_here.astype(jnp.float32)
    divisor = jnp.maximum(kept_count * tile_live[:, None] * column_live[None, :], 1.0).reshape(
        -1, 1
    )
    swapped = (
        out_weight.reshape(hidden, hidden, pair_width)
        .transpose(1, 0, 2)
        .reshape(hidden * hidden, pair_width)
    )
    pair, grad_w, grad_lt, grad_r = pair_tile(
        lt,
        right,
        swapped,
        cotangent.reshape(-1, pair_width),
        divisor,
        out_bias.reshape(1, -1),
        res_local,
        hidden,
    )
    pair_output_update = pair.reshape(tile_rows, res_local, pair_width)
    left_parts = (
        grad_lt.reshape(fold, rows, seq_local, factor, inner * hidden)
        .transpose(1, 3, 0, 2, 4)
        .reshape(rows * factor, fold, seq_local, inner * hidden)
    )
    got_left, got_right, got_w = exchange(
        [
            left_parts,
            grad_r.reshape(rows, seq_local, hidden * res_local),
            grad_w.reshape(cols, -1, pair_width),
        ],
        [route_untile, route_scatter_row, route_scatter_col],
        rows,
        cols,
        1,
    )
    grad_left = (
        jnp.sum(got_left.astype(jnp.float32), axis=0)
        .reshape(fold, seq_local, inner, hidden)
        .transpose(1, 2, 0, 3)
        .reshape(seq_local, res_local, hidden)
    )
    grad_right = (
        jnp.sum(got_right.astype(jnp.float32), axis=0)
        .reshape(seq_local, hidden, res_local)
        .transpose(0, 2, 1)
    )
    grad_w_col = jnp.sum(got_w.astype(jnp.float32), axis=0).astype(jnp.bfloat16)
    grad_projected = jnp.concatenate([grad_left, grad_right], axis=-1) * live[:, :, None]
    grad_low = grad_projected.astype(jnp.bfloat16)
    normalized_input_gradient = jnp.dot(
        grad_low.reshape(-1, 2 * hidden), proj_weight.T, preferred_element_type=jnp.float32
    ).reshape(seq_local, res_local, channels)
    weight_local = lax.dot_general(
        normed.reshape(-1, channels),
        grad_low.reshape(-1, 2 * hidden),
        (((0,), (0,)), ((), ())),
        preferred_element_type=jnp.float32,
    )
    bias_local = jnp.sum(grad_projected, axis=(0, 1))
    gain_local = jnp.sum(normalized_input_gradient * scaled_product, axis=(0, 1))
    shift_local = jnp.sum(normalized_input_gradient, axis=(0, 1))
    alignment_gradient = layer_norm_backward_pass(
        normalized_input_gradient, scaled_product, inverse_deviation, layer_norm_gain
    ).astype(jnp.bfloat16)
    vectors = jnp.stack(
        [gain_local, shift_local, jnp.pad(bias_local, (0, channels - 2 * hidden))]
    )
    row_w, row_weight, row_vectors = exchange(
        [
            grad_w_col.reshape(rows, -1, pair_width),
            weight_local.T.astype(jnp.bfloat16),
            vectors,
        ],
        [route_scatter_row, route_gather_row, route_gather_row],
        rows,
        cols,
        2,
        along_row=True,
    )
    all_w, all_weight, all_vectors = exchange(
        [
            jnp.sum(row_w.astype(jnp.float32), axis=0).astype(jnp.bfloat16),
            jnp.sum(row_weight.astype(jnp.float32), axis=0).astype(jnp.bfloat16),
            jnp.sum(row_vectors, axis=0),
        ],
        [route_gather_all, route_gather_col, route_gather_col],
        rows,
        cols,
        3,
    )
    output_weight_gradient = (
        all_w.reshape(rows, cols, -1, pair_width)
        .transpose(1, 0, 2, 3)
        .reshape(hidden, hidden, pair_width)
        .transpose(1, 0, 2)
        .reshape(hidden * hidden, pair_width)
        .astype(jnp.float32)
    )
    weight_sum = jnp.sum(all_weight.astype(jnp.float32), axis=0).T
    vector_sum = jnp.sum(all_vectors, axis=0)
    return (
        pair_output_update,
        alignment_gradient,
        vector_sum[0],
        vector_sum[1],
        weight_sum,
        vector_sum[2, : 2 * hidden],
        output_weight_gradient,
    )


def solution(mesh):
    return jax.shard_map(
        shards,
        mesh=mesh,
        in_specs=(
            P(("groups", "row"), "col", None),
            P("groups"),
            P("groups"),
            P(),
            P(),
            P(),
            P(),
            P(),
            P(),
            P(("groups", "row"), "col", None),
        ),
        out_specs=(
            P(("groups", "row"), "col", None),
            P(("groups", "row"), "col", None),
            P("groups"),
            P("groups"),
            P("groups", None),
            P("groups"),
            P("groups", None),
        ),
        check_vma=False,
    )
```

profile of v0, /device:TPU:0, one launch (start us, length us, event | category | flops | bytes accessed | tf_op | source)
XLA Modules:
  0.0 111.3 jit_solution(5561963414773482310)
XLA Ops:
  0.7 1.4 %reduce_sum.155 = s32[]{:T(128)} reduce(s32[128]{0:T(128)} %param.11, s32[]{:T(128)} %constant.26.clone.1), dimensions={0}, to_apply=%region_2.0 | reduce | flops 127 | bytes 520 | tf_op jit(solution)/shard_map/reduce_sum | solution.py:435
  2.7 0.7 convert_multiply_fusion
  5.0 1.3 %convert_reduce_fusion = f32[32,32]{1,0:T(8,128)S(1)} fusion(bf16[32,32,256]{2,1,0:T(8,128)(2,1)} %param.10), kind=kLoop, calls=%fused_computation.1 | loop fusion | flops 523264 | bytes 528384 | tf_op jit(solution)/shard_map/reduce_sum | solution.py:17
  8.3 0.8 copy.36
  9.4 0.9 reshape.185.refs_1_
  10.4 0.8 reshape.184.refs_0_
  11.2 25.0 %shard_map.153 = (bf16[4,4,32,256]{3,2,1,0:T(8,128)(2,1)}, bf16[4,32,1024]{2,1,0:T(8,128)(2,1)}) custom-call(bf16[4,32,256]{2,1,0:T(8,128)(2,1)} %reshape.184.refs_0_, bf16[32,1024]{1,0:T(8,128)(2,1)} %reshape.185.refs_1_), custom_call_target="tpu_custom_call" | custom-call | tf_op jit(solution)/shard_map/pallas_call | solution.py:227
  36.2 1.0 copy.34
  37.2 0.9 copy.35
  38.1 1.3 %max.19.div_ref = f32[1024,1]{1,0:T(8,128)} reshape(f32[32,32]{1,0:T(8,128)S(1)} %multiply_maximum_fusion) | data formatting | bytes 8192 | tf_op jit(solution)/shard_map/max | solution.py:440
  39.4 14.6 %shard_map.154 = (bf16[1024,128]{1,0:T(8,128)(2,1)}, bf16[1024,128]{1,0:T(8,128)(2,1)}, bf16[512,256]{1,0:T(8,128)(2,1)}, bf16[128,1024]{1,0:T(8,128)(2,1)}) custom-call(bf16[512,256]{1,0:T(8,128)(2,1)} %bitcast.63, bf16[256,512]{1,0:T(8,128)(2,1)} %bitcast.71, bf16[128,1024]{1,0:T(8,128)(2,1)} %bitcast.82, bf16[1024,128]{1,0:T(8,128)(2,1)} %bitcast.70, ...), custom_call_target="tpu_custom_call" | custom-call | tf_op jit(solution)/shard_map/pallas_call | solution.py:353
  54.0 1.7 %copy.45 = bf16[4,4,32,1,256]{4,2,0,1,3:T(8,128)(2,1)} copy(bf16[4,4,32,1,256]{4,2,1,0,3:T(8,128)(2,1)} %bitcast.79) | data formatting | bytes 524288 | tf_op jit(solution)/shard_map/reshape | solution.py:460
  55.7 17.4 %shard_map.155 = (bf16[4,4,32,256]{3,2,1,0:T(8,128)(2,1)}, bf16[4,32,1024]{2,1,0:T(8,128)(2,1)}, bf16[4,256,128]{2,1,0:T(8,128)(2,1)}) custom-call(bf16[4,4,32,256]{3,2,1,0:T(8,128)(2,1)} %bitcast.68, bf16[4,32,1024]{2,1,0:T(8,128)(2,1)} %bitcast.76, bf16[4,256,128]{2,1,0:T(8,128)(2,1)} %bitcast.75), custom_call_target="tpu_custom_call" | custom-call | tf_op jit(solution)/shard_map/pallas_call | solution.py:227
  73.1 1.0 convert_reduce_fusion.2
  76.4 1.2 %fusion.8.refs_1_ = bf16[64,256]{1,0:T(8,128)(2,1)} fusion(bf16[32,32,256]{2,1,0:T(8,128)(2,1)S(1)} %copy-done.1, f32[256]{0:T(256)S(1)} %copy-done.8, f32[256]{0:T(256)S(1)} %copy-done.7, f32[32,32]{1,0:T(8,128)S(1)} %add_rsqrt_fusion, f32[32,32]{1,0:T(8,128)S(1)} %broadcast_multiply_fusion.2, bf16[32,32,64]{2,1,0:T(8,128)(2,1)S(1)} %get-tuple-element.42), kind=kOutput, calls=%fused_computation.12 | convolution fusion | flops 35143680 | bytes 698368 | tf_op jit(solution)/shard_map/dot_general | solution.py:492
  77.6 0.7 fusion.15
  78.9 1.4 %fusion.14 = bf16[32,32,256]{2,1,0:T(8,128)(2,1)} fusion(bf16[32,32,256]{2,1,0:T(8,128)(2,1)S(1)} %copy-done.1, f32[32,32,256]{2,1,0:T(8,128)S(1)} %get-tuple-element.49, f32[32,32]{1,0:T(8,128)S(1)} %get-tuple-element.50, f32[32,32]{1,0:T(8,128)S(1)} %get-tuple-element.51, f32[256]{0:T(256)S(1)} %copy-done.7, f32[32,32]{1,0:T(8,128)S(1)} %add_rsqrt_fusion, ...), kind=kLoop, calls=%fused_computation.18 | loop fusion | flops 2359296 | bytes 2114560 | tf_op jit(solution)/shard_map/convert_element_type | solution.py:503
  80.3 10.7 %shard_map.156 = (bf16[4,64,128]{2,1,0:T(8,128)(2,1)}, bf16[4,64,256]{2,1,0:T(8,128)(2,1)}, f32[4,3,256]{2,1,0:T(4,128)}) custom-call(bf16[4,64,128]{2,1,0:T(8,128)(2,1)} %bitcast.77, bf16[64,256]{1,0:T(8,128)(2,1)} %fusion.8.refs_1_, f32[3,256]{1,0:T(4,128)} %pad_maximum_fusion.refs_2_), custom_call_target="tpu_custom_call" | custom-call | tf_op jit(solution)/shard_map/pallas_call | solution.py:227
  91.1 1.5 %reduce_sum.164.refs_0_ = bf16[64,128]{1,0:T(8,128)(2,1)} reduce(bf16[4,64,128]{2,1,0:T(8,128)(2,1)} %get-tuple-element.31, bf16[]{:T(256)} %constant.29.clone.1), dimensions={0}, to_apply=%region_11.12 | reduce | flops 24576 | bytes 81922 | tf_op jit(solution)/shard_map/reduce_sum | solution.py:521
  92.5 1.6 %reduce_sum.165.refs_1_ = bf16[64,256]{1,0:T(8,128)(2,1)} reduce(bf16[4,64,256]{2,1,0:T(8,128)(2,1)} %get-tuple-element.32, bf16[]{:T(256)} %constant.29.clone.1), dimensions={0}, to_apply=%region_12.13 | reduce | flops 49152 | bytes 163842 | tf_op jit(solution)/shard_map/reduce_sum | solution.py:522
  94.7 11.1 %shard_map.157 = (bf16[16,64,128]{2,1,0:T(8,128)(2,1)}, bf16[4,64,256]{2,1,0:T(8,128)(2,1)}, f32[4,3,256]{2,1,0:T(4,128)}) custom-call(bf16[64,128]{1,0:T(8,128)(2,1)} %reduce_sum.164.refs_0_, bf16[64,256]{1,0:T(8,128)(2,1)} %reduce_sum.165.refs_1_, f32[3,256]{1,0:T(4,128)} %reduce_sum.166.refs_2_), custom_call_target="tpu_custom_call" | custom-call | tf_op jit(solution)/shard_map/pallas_call | solution.py:227
  107.7 1.6 %convert_reduce_fusion.3 = f32[64,256]{1,0:T(8,128)} fusion(bf16[4,64,256]{2,1,0:T(8,128)(2,1)} %get-tuple-element.35), kind=kLoop, calls=%fused_computation.28 | loop fusion | flops 114688 | bytes 196608 | tf_op jit(solution)/shard_map/reduce_sum | solution.py:538
  109.2 1.0 copy.41
  110.2 1.1 copy.42
  (45 shorter events, 9.2 us)
Async XLA Ops:
  0.6 6.1 %copy-start = (bf16[256,64]{0,1:T(8,128)(2,1)S(1)}, bf16[256,64]{0,1:T(8,128)(2,1)}, u32[]{:S(2)}) copy-start(bf16[256,64]{0,1:T(8,128)(2,1)} %param.15) | copy-start | bytes 98308
  0.6 5.6 %copy-start.1 = (bf16[32,32,256]{2,1,0:T(8,128)(2,1)S(1)}, bf16[32,32,256]{2,1,0:T(8,128)(2,1)}, u32[]{:S(2)}) copy-start(bf16[32,32,256]{2,1,0:T(8,128)(2,1)} %param.10) | copy-start | bytes 1572868
  6.7 0.7 copy-start.7
  6.7 0.7 copy-start.8
  6.7 0.7 copy-start.9
  7.4 1.0 copy-start.5
  37.2 0.9 copy-start.2
  73.1 1.1 copy-start.3
  74.1 1.0 copy-start.4
  92.5 1.6 %copy-start.6 = (f32[4,3,256]{2,1,0:T(4,128)S(1)}, f32[4,3,256]{2,1,0:T(4,128)}, u32[]{:S(2)}) copy-start(f32[4,3,256]{2,1,0:T(4,128)} %get-tuple-element.33) | copy-start | bytes 36868
where the time goes:
time: 112 us; the launch traced here: 111 us
  Pallas kernels  78.9 us (70%)
  other arithmetic  14.6 us (13%)
  local copies, waits for them, and re-layouts  14 us (12%)
  matrix products  2.37 us (2%)
  between operations  1.52 us (1%)
    pallas_call x4, Pallas kernels, exchange(): pl.pallas_call(functools.partial(exchange_kernel, routes, rows, cols, alo...  64.3 us
    pallas_call x1, Pallas kernels, pair_tile(): pl.pallas_call(functools.partial(pair_kernel, res, hidden), grid=(hidden...  14.6 us

commit v1 on v0

v1 whole, which is shorter than its diff:
```python
import functools

import jax
import jax.numpy as jnp
from jax import lax
from jax.experimental import pallas as pl
from jax.experimental.pallas import tpu as pltpu
from jax.sharding import PartitionSpec as P

EPSILON = 1e-05
LANES = 128
WIDE = 256
MESH = pl.DeviceIdType.MESH
F32 = jnp.float32
BF16 = jnp.bfloat16


def lane_group_swap(blocks, width):
    lane = lax.broadcasted_iota(jnp.int32, blocks[0].shape, 1)
    span = len(blocks) // 2
    while span:
        low = (lane // (width * span)) % 2 == 0
        out = list(blocks)
        for a in range(len(blocks)):
            if a & span:
                continue
            first, second = blocks[a], blocks[a + span]
            shift = width * span
            out[a] = jnp.where(low, first, pltpu.roll(second, shift, 1))
            out[a + span] = jnp.where(low, pltpu.roll(first, LANES - shift, 1), second)
        blocks = out
        span //= 2
    return blocks


def place_groups(pieces, shifts, width):
    group = lax.broadcasted_iota(jnp.int32, pieces[0].shape, 1) // width
    out = None
    for k, (piece, shift) in enumerate(zip(pieces, shifts)):
        rolled = pltpu.roll(piece, shift % LANES, 1) if shift % LANES else piece
        out = rolled if out is None else jnp.where(group == k, rolled, out)
    return out


def nt(a, b):
    return lax.dot_general(a, b, (((1,), (1,)), ((), ())), preferred_element_type=F32)


def tn(a, b):
    return lax.dot_general(a, b, (((0,), (0,)), ((), ())), preferred_element_type=F32)


def nn(a, b):
    return jnp.dot(a, b, preferred_element_type=F32)


def aligned(start, size, step=None):
    return pl.ds(pl.multiple_of(start, step or size), size)


def fused_kernel(dims, *refs):
    rows, cols, seq_local, res_local, hidden, channels, width = dims
    (x_hbm, seq_ref, res_ref, gain_ref, shift_ref, w_ref, pb_ref, ow_hbm, ob_ref, cot_hbm) = refs[:10]
    (pair_hbm, ag_hbm, gw_ref, gpw_ref, vec_ref) = refs[10:15]
    (
        x_ref,
        ow_ref,
        cot_ref,
        pair_ref,
        ag_ref,
        scaled_ref,
        inv_ref,
        normed_ref,
        prj_ref,
        tr_ref,
        u_ref,
        seqcol_ref,
        lsend_ref,
        lbuf_ref,
        rbuf_ref,
        owf_ref,
        wp_ref,
        gpre_ref,
        gp_ref,
        prod_ref,
        gls_ref,
        glr_ref,
        glmid_ref,
        glfin_ref,
        grs_ref,
        grr_ref,
        gws_ref,
        gwr_ref,
        gwc_ref,
        gwcr_ref,
        gwg_ref,
        low_ref,
        sw_ref,
        swr_ref,
        swc_ref,
        swcr_ref,
        sv_ref,
        svr_ref,
        svc_ref,
        svcr_ref,
        local_sems,
        one_sems,
        col_send,
        col_recv,
        row_send,
        row_recv,
    ) = refs[15:]
    r = lax.axis_index("row")
    c = lax.axis_index("col")
    factor = cols // rows
    seqs = seq_local * rows
    tile_rows = res_local * factor
    n = seq_local * res_local
    pairs = tile_rows * res_local
    block = res_local * hidden
    fold = LANES // res_local
    chunks = n // LANES
    majors = block // LANES
    total = rows * cols
    barrier = pltpu.get_barrier_semaphore()

    def greet(t, carry):
        other = lax.rem(r * cols + c + t, total)
        pl.semaphore_signal(
            barrier,
            inc=1,
            device_id={"row": other // cols, "col": lax.rem(other, cols)},
            device_id_type=MESH,
        )
        return carry

    lax.fori_loop(1, total, greet, 0)
    load_x = pltpu.make_async_copy(x_hbm, x_ref, local_sems.at[0])
    load_w = pltpu.make_async_copy(ow_hbm, ow_ref, local_sems.at[1])
    load_c = pltpu.make_async_copy(cot_hbm, cot_ref, local_sems.at[2])
    load_x.start()
    load_w.start()
    load_c.start()

    def remote(src, dst, send_sem, recv_sem, trow, tcol):
        return pltpu.make_async_remote_copy(
            src_ref=src,
            dst_ref=dst,
            send_sem=send_sem,
            recv_sem=recv_sem,
            device_id={"row": trow, "col": tcol},
            device_id_type=MESH,
        )

    def over(kind, plane):
        if kind == "col":
            return cols, c, col_send.at[plane], col_recv.at[plane], lambda k: (r, k)
        return rows, r, row_send.at[plane], row_recv.at[plane], lambda k: (k, c)

    def start(kind, plane, src, dst):
        count, me, send, recv, where = over(kind, plane)

        def body(t, carry):
            k = lax.rem(me + t, count)
            remote(src(k), dst(me), send.at[k], recv.at[me], *where(k)).start()
            return carry

        lax.fori_loop(1, count, body, 0)

    def receive(kind, plane, src, dst):
        count, me, send, recv, where = over(kind, plane)

        def body(t, carry):
            k = lax.rem(me + t, count)
            remote(dst(k), dst(k), send.at[k], recv.at[k], *where(k)).wait_recv()
            return carry

        lax.fori_loop(1, count, body, 0)

    def drain(kind, plane, src, dst):
        count, me, send, recv, where = over(kind, plane)

        def body(t, carry):
            k = lax.rem(me + t, count)
            remote(src(k), dst(me), send.at[k], recv.at[me], *where(k)).wait_send()
            return carry

        lax.fori_loop(1, count, body, 0)

    def column(mask_ref, count, offset):
        size = mask_ref.shape[1]
        shape = (count, size)
        hit = lax.broadcasted_iota(jnp.int32, shape, 1) == lax.broadcasted_iota(jnp.int32, shape, 0) + offset
        values = jnp.broadcast_to(mask_ref[...].astype(F32), shape)
        return jnp.sum(jnp.where(hit, values, 0.0), axis=1, keepdims=True)

    seqcol_ref[...] = jnp.broadcast_to(column(seq_ref, seq_local, r * seq_local), seqcol_ref.shape)
    rescol = column(res_ref, res_local, c * res_local)
    tilecol = column(res_ref, tile_rows, r * tile_rows)
    kept = jnp.sum(seq_ref[...].astype(F32), axis=1, keepdims=True)

    def live_column(k):
        parts = []
        for q in range(fold):
            parts.append(rescol * seqcol_ref[pl.ds(k * fold + q, 1), 0:1])
        return jnp.concatenate(parts, axis=0)

    w = w_ref[...].astype(F32)
    w = jnp.concatenate([w, jnp.zeros((channels, LANES - 2 * hidden), F32)], axis=1)
    w_wide = w.astype(BF16)
    w_turned = w.T.astype(BF16)
    bias = pb_ref[...]
    bias = jnp.concatenate([bias, jnp.zeros((1, LANES - 2 * hidden), F32)], axis=1)
    gain = gain_ref[...]
    shift = shift_ref[...]

    load_x.wait()

    def layer_norm(k, carry):
        here = aligned(k * LANES, LANES)
        widened = x_ref[here, :].astype(F32)
        centred = widened - jnp.mean(widened, axis=-1, keepdims=True)
        inverse = lax.rsqrt(jnp.mean(centred * centred, axis=-1, keepdims=True) + EPSILON)
        scaled = centred * inverse
        normed = (scaled * gain + shift).astype(BF16)
        scaled_ref[here, :] = scaled
        inv_ref[here, :] = inverse
        normed_ref[here, :] = normed
        prj = (nn(normed, w_wide) + bias) * live_column(k)
        prj_ref[here, :] = prj
        tr_ref[here, :] = prj.T
        return carry

    lax.fori_loop(0, chunks, layer_norm, 0)

    for im in range(majors):
        pieces = [prj_ref[pl.ds(im * fold + k, seq_local, stride=res_local), :] for k in range(fold)]
        left = place_groups(pieces, [k * hidden for k in range(fold)], hidden)
        lsend_ref[:, im * LANES : (im + 1) * LANES] = left.astype(BF16)
    for sb in range(chunks):
        pieces = [
            tr_ref[pl.ds(sb * LANES + hidden + k, majors, stride=fold), :] for k in range(fold)
        ]
        for q in range(fold):
            turned = place_groups(pieces, [(k - q) * res_local for k in range(fold)], res_local)
            u_ref[pl.ds(sb * fold + q, majors, stride=seq_local), :] = turned
    my_seqs = aligned(r * seq_local, seq_local)
    for dm in range(majors):
        rbuf_ref[my_seqs, dm * LANES : (dm + 1) * LANES] = u_ref[
            dm * seq_local : (dm + 1) * seq_local, :
        ].astype(BF16)

    pl.semaphore_wait(barrier, total - 1)

    def left_slot(k):
        return lbuf_ref.at[aligned((k // factor) * seq_local, seq_local), aligned(lax.rem(k, factor) * block, block)]

    relay_row = c // factor
    relay_col = r * factor + lax.rem(c, factor)
    at_home = jnp.logical_and(relay_row == r, relay_col == c)
    left_out = remote(
        lsend_ref, left_slot(relay_col), one_sems.at[0], one_sems.at[1], relay_row, relay_col
    )
    left_home = pltpu.make_async_copy(lsend_ref, left_slot(c), local_sems.at[3])

    @pl.when(at_home)
    def _():
        left_home.start()

    @pl.when(jnp.logical_not(at_home))
    def _():
        left_out.start()

    def right_block(k):
        return rbuf_ref.at[aligned(k * seq_local, seq_local), :]

    right_args = ("row", 0, lambda k: right_block(r), right_block)
    start(*right_args)

    load_w.wait()
    load_c.wait()
    owf_ref[...] = ow_ref[...].astype(F32)
    for d in range(hidden):
        wp_ref[d * hidden : (d + 1) * hidden, :] = owf_ref[pl.ds(d, hidden, stride=hidden), :].astype(BF16)

    def inverse_divisor(i):
        return 1.0 / jnp.maximum(kept * tilecol[i : i + 1, :] * rescol, 1.0)

    for i in range(tile_rows):
        here = slice(i * res_local, (i + 1) * res_local)
        gpre_ref[here, :] = (cot_ref[here, :].astype(F32) * inverse_divisor(i)).astype(BF16)

    half = WIDE // LANES

    def grad_products(ip, carry):
        upstream = gpre_ref[aligned(ip * WIDE, WIDE), :]
        for dm in range(majors):
            tile = nt(wp_ref[dm * LANES : (dm + 1) * LANES, :], upstream)
            for h in range(half):
                blocks = [
                    tile[a * hidden : (a + 1) * hidden, h * LANES : (h + 1) * LANES] for a in range(fold)
                ]
                for a, swapped in enumerate(lane_group_swap(blocks, res_local)):
                    gp_ref[
                        aligned(((ip * half + h) * fold + a) * hidden, hidden), dm * LANES : (dm + 1) * LANES
                    ] = swapped.astype(BF16)
        return carry

    steps = pairs // WIDE
    lax.fori_loop(0, steps // 2, grad_products, 0)

    @pl.when(at_home)
    def _():
        left_home.wait()

    @pl.when(jnp.logical_not(at_home))
    def _():
        remote(
            left_slot(c), left_slot(c), one_sems.at[0], one_sems.at[1], relay_row, relay_col
        ).wait_recv()

    left_args = ("col", 0, lambda k: left_slot(c), left_slot)
    start(*left_args)
    lax.fori_loop(steps // 2, steps, grad_products, 0)
    receive(*right_args)
    receive(*left_args)

    def gl_part(k):
        return gls_ref.at[aligned((k // factor) * seq_local, seq_local), aligned(lax.rem(k, factor) * block, block)]

    for k in range(tile_rows * hidden // WIDE):
        gls_ref[:, k * WIDE : (k + 1) * WIDE] = nt(rbuf_ref[...], gp_ref[k * WIDE : (k + 1) * WIDE, :]).astype(BF16)
    gl_args = ("col", 1, gl_part, lambda k: glr_ref.at[k])
    start(*gl_args)
    for k in range(block // WIDE):
        grs_ref[:, k * WIDE : (k + 1) * WIDE] = nn(lbuf_ref[...], gp_ref[:, k * WIDE : (k + 1) * WIDE]).astype(BF16)
    gr_args = (
        "row",
        1,
        lambda k: grs_ref.at[aligned(k * seq_local, seq_local), :],
        lambda k: grr_ref.at[k],
    )
    start(*gr_args)

    def products(im, carry):
        left = lbuf_ref[:, aligned(im * LANES, LANES)]
        for k in range(block // WIDE):
            tile = tn(left, rbuf_ref[:, k * WIDE : (k + 1) * WIDE])
            for h in range(half):
                blocks = [
                    tile[a * hidden : (a + 1) * hidden, h * LANES : (h + 1) * LANES] for a in range(fold)
                ]
                for a, swapped in enumerate(lane_group_swap(blocks, res_local)):
                    at = ((k * half + h) * fold + a) * hidden
                    prod_ref[at : at + hidden, aligned(im * LANES, LANES)] = swapped.astype(BF16)
        return carry

    steps = tile_rows // fold
    lax.fori_loop(0, steps // 2, products, 0)

    receive(*gl_args)
    mine = gls_ref[aligned((c // factor) * seq_local, seq_local), aligned(lax.rem(c, factor) * block, block)]

    def add_left(t, carry):
        return carry + glr_ref[lax.rem(c + t, cols)].astype(F32)

    glmid_ref[...] = lax.fori_loop(1, cols, add_left, mine.astype(F32)).astype(BF16)
    gl_out = remote(glmid_ref, glfin_ref, one_sems.at[2], one_sems.at[3], relay_row, relay_col)
    gl_home = pltpu.make_async_copy(glmid_ref, glfin_ref, local_sems.at[4])

    @pl.when(at_home)
    def _():
        gl_home.start()

    @pl.when(jnp.logical_not(at_home))
    def _():
        gl_out.start()

    lax.fori_loop(steps // 2, steps, products, 0)

    for k in range(hidden * hidden // WIDE):
        owf_ref[k * WIDE : (k + 1) * WIDE, :] = nn(prod_ref[k * WIDE : (k + 1) * WIDE, :], gpre_ref[...])
    for k in range(hidden):
        gws_ref[k * hidden : (k + 1) * hidden, :] = owf_ref[pl.ds(k, hidden, stride=hidden), :].astype(BF16)
    w_block = hidden * hidden // cols
    gw_row_args = (
        "col",
        2,
        lambda k: gws_ref.at[aligned(k * w_block, w_block), :],
        lambda k: gwr_ref.at[k],
    )
    start(*gw_row_args)

    out_bias = ob_ref[...]
    for k in range(pairs // WIDE):
        pre = tn(wp_ref[...], prod_ref[:, k * WIDE : (k + 1) * WIDE]).T + out_bias
        for q in range(WIDE // res_local):
            i = k * (WIDE // res_local) + q
            pair_ref[i * res_local : (i + 1) * res_local, :] = (
                pre[q * res_local : (q + 1) * res_local, :] * inverse_divisor(i)
            ).astype(BF16)
    store_pair = pltpu.make_async_copy(pair_ref, pair_hbm, local_sems.at[5])
    store_pair.start()

    w_small = w_block // rows
    receive(*gw_row_args)
    summed = gws_ref[aligned(c * w_block, w_block), :].astype(F32)

    def add_w(t, carry):
        return carry + gwr_ref[lax.rem(c + t, cols)].astype(F32)

    summed = lax.fori_loop(1, cols, add_w, summed).astype(BF16)
    for k in range(rows):
        gwc_ref[k] = summed[k * w_small : (k + 1) * w_small, :]
    gw_col_args = ("row", 2, lambda k: gwc_ref.at[k], lambda k: gwcr_ref.at[k])
    start(*gw_col_args)

    receive(*gr_args)
    for dm in range(majors):
        part = slice(dm * LANES, (dm + 1) * LANES)
        total_right = grs_ref[my_seqs, part].astype(F32)

        def add_right(t, carry, part=part):
            return carry + grr_ref[lax.rem(r + t, rows), :, part].astype(F32)

        u_ref[dm * seq_local : (dm + 1) * seq_local, :] = lax.fori_loop(1, rows, add_right, total_right)
    for sb in range(chunks):
        pieces = [u_ref[pl.ds(sb * fold + q, majors, stride=seq_local), :] for q in range(fold)]
        for k in range(fold):
            turned = place_groups(pieces, [(q - k) * res_local for q in range(fold)], res_local)
            tr_ref[pl.ds(sb * LANES + hidden + k, majors, stride=fold), :] = turned

    @pl.when(at_home)
    def _():
        gl_home.wait()

    @pl.when(jnp.logical_not(at_home))
    def _():
        remote(glmid_ref, glfin_ref, one_sems.at[2], one_sems.at[3], relay_row, relay_col).wait_recv()

    for im in range(majors):
        piece = glfin_ref[:, im * LANES : (im + 1) * LANES].astype(F32)
        for k in range(fold):
            rolled = pltpu.roll(piece, LANES - k * hidden, 1) if k else piece
            prj_ref[pl.ds(im * fold + k, seq_local, stride=res_local), :] = rolled

    lane = lax.broadcasted_iota(jnp.int32, (LANES, LANES), 1)

    def backward(k, carry):
        bias_sum, gain_sum, shift_sum = carry
        here = aligned(k * LANES, LANES)
        projected = jnp.where(lane < hidden, prj_ref[here, :], tr_ref[here, :].T)
        projected = jnp.where(lane < 2 * hidden, projected * live_column(k), 0.0)
        low = projected.astype(BF16)
        low_ref[here, :] = low
        upstream = nn(low, w_turned)
        scaled = scaled_ref[here, :]
        bias_sum = bias_sum + jnp.sum(projected, axis=0, keepdims=True)
        gain_sum = gain_sum + jnp.sum(upstream * scaled, axis=0, keepdims=True)
        shift_sum = shift_sum + jnp.sum(upstream, axis=0, keepdims=True)
        grad_scaled = upstream * gain
        first = jnp.mean(grad_scaled, axis=-1, keepdims=True)
        second = jnp.mean(grad_scaled * scaled, axis=-1, keepdims=True)
        ag_ref[here, :] = (inv_ref[here, :] * (grad_scaled - first - scaled * second)).astype(BF16)
        return bias_sum, gain_sum, shift_sum

    bias_sum, gain_sum, shift_sum = lax.fori_loop(
        0,
        chunks,
        backward,
        (jnp.zeros((1, LANES), F32), jnp.zeros((1, channels), F32), jnp.zeros((1, channels), F32)),
    )
    store_ag = pltpu.make_async_copy(ag_ref, ag_hbm, local_sems.at[6])
    store_ag.start()
    sw_ref[...] = tn(low_ref[...], normed_ref[...])[: 2 * hidden, :].astype(BF16)
    sv_ref[0:1, :] = gain_sum
    sv_ref[1:2, :] = shift_sum
    sv_ref[2:3, :] = jnp.concatenate([bias_sum, jnp.zeros((1, channels - LANES), F32)], axis=1)
    sv_ref[3:8, :] = jnp.zeros((5, channels), F32)
    sw_row_args = ("col", 3, lambda k: sw_ref, lambda k: swr_ref.at[k])
    sv_row_args = ("col", 4, lambda k: sv_ref, lambda k: svr_ref.at[k])
    start(*sw_row_args)
    start(*sv_row_args)

    receive(*gw_col_args)

    def add_w_col(t, carry):
        return carry + gwcr_ref[lax.rem(r + t, rows)].astype(F32)

    gwg_ref[r] = lax.fori_loop(1, rows, add_w_col, gwc_ref[r].astype(F32)).astype(BF16)
    gw_up_args = ("row", 3, lambda k: gwg_ref.at[r], lambda k: gwg_ref.at[k])
    start(*gw_up_args)

    receive(*sw_row_args)
    receive(*sv_row_args)

    def add_sw(t, carry):
        return carry + swr_ref[lax.rem(c + t, cols)].astype(F32)

    def add_sv(t, carry):
        return carry + svr_ref[lax.rem(c + t, cols)]

    swc_ref[...] = lax.fori_loop(1, cols, add_sw, sw_ref[...].astype(F32)).astype(BF16)
    svc_ref[...] = lax.fori_loop(1, cols, add_sv, sv_ref[...])
    sw_col_args = ("row", 4, lambda k: swc_ref, lambda k: swcr_ref.at[k])
    sv_col_args = ("row", 5, lambda k: svc_ref, lambda k: svcr_ref.at[k])
    start(*sw_col_args)
    start(*sv_col_args)

    receive(*gw_up_args)
    gw_ref[c] = gwg_ref[...]
    gw_out_args = ("col", 5, lambda k: gwg_ref, lambda k: gw_ref.at[k])
    start(*gw_out_args)

    receive(*sw_col_args)
    receive(*sv_col_args)

    def add_swc(t, carry):
        return carry + swcr_ref[t].astype(F32)

    def add_svc(t, carry):
        return carry + svcr_ref[t]

    swcr_ref[r] = swc_ref[...]
    svcr_ref[r] = svc_ref[...]
    gpw_ref[...] = lax.fori_loop(0, rows, add_swc, jnp.zeros(gpw_ref.shape, F32))
    vec_ref[...] = lax.fori_loop(0, rows, add_svc, jnp.zeros(vec_ref.shape, F32))
    receive(*gw_out_args)

    @pl.when(jnp.logical_not(at_home))
    def _():
        left_out.wait_send()
        gl_out.wait_send()

    for args in (
        right_args,
        left_args,
        gl_args,
        gr_args,
        gw_row_args,
        gw_col_args,
        sw_row_args,
        sv_row_args,
        gw_up_args,
        sw_col_args,
        sv_col_args,
        gw_out_args,
    ):
        drain(*args)
    store_pair.wait()
    store_ag.wait()


def shards(
    alignment,
    sequence_mask,
    residue_mask,
    layer_norm_gain,
    norm_shift,
    proj_weight,
    proj_bias,
    out_weight,
    out_bias,
    cotangent,
):
    rows = lax.axis_size("row")
    cols = lax.axis_size("col")
    factor = cols // rows
    seq_local, res_local, channels = alignment.shape
    seqs = seq_local * rows
    hidden = proj_weight.shape[1] // 2
    width = out_weight.shape[1]
    tile_rows = res_local * factor
    n = seq_local * res_local
    pairs = tile_rows * res_local
    block = res_local * hidden
    majors = block // LANES
    inner = tile_rows * hidden
    w_block = hidden * hidden // cols
    w_small = w_block // rows
    dims = (rows, cols, seq_local, res_local, hidden, channels, width)
    vmem = pl.BlockSpec(memory_space=pltpu.VMEM)
    anywhere = pl.BlockSpec(memory_space=pl.ANY)
    pair, grad_alignment, grad_w, grad_pw, vectors = pl.pallas_call(
        functools.partial(fused_kernel, dims),
        out_shape=[
            jax.ShapeDtypeStruct((pairs, width), BF16),
            jax.ShapeDtypeStruct((n, channels), BF16),
            jax.ShapeDtypeStruct((cols, rows, w_small, width), BF16),
            jax.ShapeDtypeStruct((2 * hidden, channels), F32),
            jax.ShapeDtypeStruct((8, channels), F32),
        ],
        in_specs=[anywhere, vmem, vmem, vmem, vmem, vmem, vmem, anywhere, vmem, anywhere],
        out_specs=[anywhere, anywhere, vmem, vmem, vmem],
        scratch_shapes=[
            pltpu.VMEM((n, channels), BF16),
            pltpu.VMEM((hidden * hidden, width), BF16),
            pltpu.VMEM((pairs, width), BF16),
            pltpu.VMEM((pairs, width), BF16),
            pltpu.VMEM((n, channels), BF16),
            pltpu.VMEM((n, channels), F32),
            pltpu.VMEM((n, 1), F32),
            pltpu.VMEM((n, channels), BF16),
            pltpu.VMEM((n, LANES), F32),
            pltpu.VMEM((n, LANES), F32),
            pltpu.VMEM((majors * seq_local, LANES), F32),
            pltpu.VMEM((seq_local, LANES), F32),
            pltpu.VMEM((seq_local, block), BF16),
            pltpu.VMEM((seqs, inner), BF16),
            pltpu.VMEM((seqs, block), BF16),
            pltpu.VMEM((hidden * hidden, width), F32),
            pltpu.VMEM((hidden * hidden, width), BF16),
            pltpu.VMEM((pairs, width), BF16),
            pltpu.VMEM((inner, block), BF16),
            pltpu.VMEM((hidden * hidden, pairs), BF16),
            pltpu.VMEM((seqs, inner), BF16),
            pltpu.VMEM((cols, seq_local, block), BF16),
            pltpu.VMEM((seq_local, block), BF16),
            pltpu.VMEM((seq_local, block), BF16),
            pltpu.VMEM((seqs, block), BF16),
            pltpu.VMEM((rows, seq_local, block), BF16),
            pltpu.VMEM((hidden * hidden, width), BF16),
            pltpu.VMEM((cols, w_block, width), BF16),
            pltpu.VMEM((rows, w_small, width), BF16),
            pltpu.VMEM((rows, w_small, width), BF16),
            pltpu.VMEM((rows, w_small, width), BF16),
            pltpu.VMEM((n, LANES), BF16),
            pltpu.VMEM((2 * hidden, channels), BF16),
            pltpu.VMEM((cols, 2 * hidden, channels), BF16),
            pltpu.VMEM((2 * hidden, channels), BF16),
            pltpu.VMEM((rows, 2 * hidden, channels), BF16),
            pltpu.VMEM((8, channels), F32),
            pltpu.VMEM((cols, 8, channels), F32),
            pltpu.VMEM((8, channels), F32),
            pltpu.VMEM((rows, 8, channels), F32),
            pltpu.SemaphoreType.DMA((7,)),
            pltpu.SemaphoreType.DMA((4,)),
            pltpu.SemaphoreType.DMA((6, cols)),
            pltpu.SemaphoreType.DMA((6, cols)),
            pltpu.SemaphoreType.DMA((6, rows)),
            pltpu.SemaphoreType.DMA((6, rows)),
        ],
        compiler_params=pltpu.CompilerParams(
            collective_id=0, has_side_effects=True, vmem_limit_bytes=48 * 1024 * 1024
        ),
    )(
        alignment.reshape(n, channels),
        sequence_mask.reshape(1, -1),
        residue_mask.reshape(1, -1),
        layer_norm_gain.reshape(1, -1),
        norm_shift.reshape(1, -1),
        proj_weight,
        proj_bias.reshape(1, -1),
        out_weight,
        out_bias.reshape(1, -1),
        cotangent.reshape(pairs, width),
    )
    return (
        pair.reshape(tile_rows, res_local, width),
        grad_alignment.reshape(seq_local, res_local, channels),
        vectors[0],
        vectors[1],
        grad_pw.T,
        vectors[2, : 2 * hidden],
        grad_w.reshape(hidden * hidden, width).astype(F32),
    )


def solution(mesh):
    return jax.shard_map(
        shards,
        mesh=mesh,
        in_specs=(
            P(("groups", "row"), "col", None),
            P("groups"),
            P("groups"),
            P(),
            P(),
            P(),
            P(),
            P(),
            P(),
            P(("groups", "row"), "col", None),
        ),
        out_specs=(
            P(("groups", "row"), "col", None),
            P(("groups", "row"), "col", None),
            P("groups"),
            P("groups"),
            P("groups", None),
            P("groups"),
            P("groups", None),
        ),
        check_vma=False,
    )
```

time: 112 us -> 54.2 us (0.48)
  Pallas kernels: 78.9 us -> 44.9 us
  other arithmetic: 14.6 us -> 0.84 us
  local copies, waits for them, and re-layouts: 14 us -> 7.07 us
  matrix products: 2.37 us -> 0 us
    pallas_call x5 -> x1, Pallas kernels: 78.9 us -> 44.9 us  [shards(): pl.pallas_call(functools.partial(fused_kernel, dims), out_shape=[jax.Shap...]
    reduce_sum x12 -> x0, other arithmetic: 11 us -> none  [the longest x1 1.56 us: shards(): jnp.sum(row_weight.astype(jnp.float32), axis=0).astype(jnp.bfloat16)]
    reshape x9 -> x0, local copies, waits for them, and re-layouts: 5.66 us -> none  [the longest x1 1.67 us: shards(): grad_lt.reshape(fold, rows, seq_local, factor, inner * hidden)]
    unnamed x20 -> x22, local copies, waits for them, and re-layouts: 1.44 us -> 5.99 us
    dot_general x3 -> x0, matrix products: 2.37 us -> none  [the longest x1 1.16 us: shards(): lax.dot_general(normed.reshape(-1, channels), grad_low.reshape(-1, 2 * hi...]
    convert_element_type x2 -> x0, local copies, waits for them, and re-layouts: 2.09 us -> none  [shards(): output_weight_gradient = all_w.reshape(rows, cols, -1, pair_width).transp...]
    transpose x4 -> x0, local copies, waits for them, and re-layouts: 1.61 us -> none  [the longest x1 0.97 us: shards(): lt = lefts.reshape(rows, factor, fold, seq_local, inner * hidden).transpo...]
    convert_element_type x3 -> x1, other arithmetic: 2.2 us -> 0.84 us  [shards(): grad_w.reshape(hidden * hidden, width).astype(F32)]
where the time goes in v1:
time: 54.2 us; the launch traced here: 53.6 us
  Pallas kernels  44.9 us (83%)
  local copies, waits for them, and re-layouts  7.07 us (13%)
  other arithmetic  0.84 us (2%)
  between operations  0.75 us (1%)
    pallas_call x1, Pallas kernels, shards(): pl.pallas_call(functools.partial(fused_kernel, dims), out_shape=[jax.Shap...  44.9 us
    unnamed x22, local copies, waits for them, and re-layouts  5.99 us

profile of v1, /device:TPU:0, one launch (start us, length us, event | category | flops | bytes accessed | tf_op | source)
XLA Modules:
  0.0 53.6 jit_solution(12053632801468573478)
XLA Ops:
  0.6 0.0 copy-start.3
  0.6 0.0 copy-start.4
  0.7 0.0 copy-start.5
  0.7 0.0 copy-start.6
  0.7 0.0 copy-start.7
  0.7 0.0 copy-start.8
  0.7 0.9 %copy.17.refs_5_ = bf16[256,64]{1,0:T(8,128)(2,1)S(1)} copy(bf16[256,64]{0,1:T(8,128)(2,1)} %param.15) | data formatting | bytes 65536 | tf_op args[5]
  1.6 0.0 copy-done.3
  1.6 0.0 copy-done.4
  1.6 0.0 copy-done.5
  1.6 0.0 copy-done.6
  1.6 0.0 copy-done.7
  1.7 0.0 copy-done.8
  1.7 0.0 copy-start
  1.7 1.0 %copy-done = bf16[32,32,256]{2,1,0:T(8,128)(2,1)S(1)} copy-done((bf16[32,32,256]{2,1,0:T(8,128)(2,1)S(1)}, bf16[32,32,256]{2,1,0:T(8,128)(2,1)}, u32[]{:S(2)}) %copy-start) | copy-done | bytes 524312
  2.7 0.9 %copy-done.1 = bf16[1024,128]{1,0:T(8,128)(2,1)S(1)} copy-done((bf16[1024,128]{1,0:T(8,128)(2,1)S(1)}, bf16[1024,128]{1,0:T(8,128)(2,1)}, u32[]{:S(2)}) %copy-start.1) | copy-done | bytes 262168
  3.7 0.9 %copy-done.2 = bf16[32,32,128]{2,1,0:T(8,128)(2,1)S(1)} copy-done((bf16[32,32,128]{2,1,0:T(8,128)(2,1)S(1)}, bf16[32,32,128]{2,1,0:T(8,128)(2,1)}, u32[]{:S(2)}) %copy-start.2) | copy-done | bytes 262168
  4.6 44.9 %shard_map.153 = (bf16[1024,128]{1,0:T(8,128)(2,1)S(1)}, bf16[1024,256]{1,0:T(8,128)(2,1)S(1)}, bf16[4,4,64,128]{3,2,1,0:T(8,128)(2,1)S(1)}, f32[64,256]{1,0:T(8,128)S(1)}, f32[8,256]{1,0:T(8,128)S(1)}) custom-call(bf16[1024,256]{1,0:T(8,128)(2,1)S(1)} %bitcast.18, s32[1,128]{1,0:T(1,128)S(1)} %bitcast.25, s32[1,128]{1,0:T(1,128)S(1)} %bitcast.26, ...), custom_call_target="tpu_custom_call" | custom-call | tf_op jit(solution)/shard_map/pallas_call | solution.py:584
  49.5 0.5 slice_bitcast_fusion
  50.1 0.6 %fusion = (f32[1,256]{1,0:T(1,128)}, f32[1,256]{1,0:T(1,128)}) fusion(f32[8,256]{1,0:T(8,128)S(1)} %get-tuple-element.14), kind=kLoop, calls=%fused_computation.2 | loop fusion | bytes 4096 | tf_op jit(solution)/shard_map/slice | solution.py:662
  50.6 0.8 %bitcast_convert_fusion = f32[1024,128]{1,0:T(8,128)} fusion(bf16[4,4,64,128]{3,2,1,0:T(8,128)(2,1)S(1)} %get-tuple-element.16), kind=kLoop, calls=%fused_computation | loop fusion | flops 131072 | bytes 786432 | tf_op jit(solution)/shard_map/convert_element_type | solution.py:665
  51.5 0.7 %copy.21 = bf16[32,32,128]{2,1,0:T(8,128)(2,1)} copy(bf16[32,32,128]{2,1,0:T(8,128)(2,1)S(1)} %bitcast.21) | data formatting | bytes 524288
  52.2 0.8 %copy.22 = bf16[32,32,256]{2,1,0:T(8,128)(2,1)} copy(bf16[32,32,256]{2,1,0:T(8,128)(2,1)S(1)} %bitcast.19) | data formatting | bytes 1048576
  53.0 0.6 %copy.23 = f32[256,64]{0,1:T(8,128)} copy(f32[256,64]{0,1:T(8,128)S(1)} %bitcast.22) | data formatting | bytes 131072
  (2 shorter events, 0.0 us)
Async XLA Ops:
  0.6 1.0 %copy-start.3 = (f32[256]{0:T(256)S(1)}, f32[256]{0:T(256)}, u32[]{:S(2)}) copy-start(f32[256]{0:T(256)} %param.13) | copy-start | bytes 3076
  0.6 1.0 %copy-start.4 = (f32[256]{0:T(256)S(1)}, f32[256]{0:T(256)}, u32[]{:S(2)}) copy-start(f32[256]{0:T(256)} %param.14) | copy-start | bytes 3076
  0.7 1.0 %copy-start.5 = (s32[128]{0:T(128)S(1)}, s32[128]{0:T(128)}, u32[]{:S(2)}) copy-start(s32[128]{0:T(128)} %param.11) | copy-start | bytes 1540
  0.7 1.0 %copy-start.6 = (s32[128]{0:T(128)S(1)}, s32[128]{0:T(128)}, u32[]{:S(2)}) copy-start(s32[128]{0:T(128)} %param.12) | copy-start | bytes 1540
  0.7 1.0 %copy-start.7 = (f32[64]{0:T(128)S(1)}, f32[64]{0:T(128)}, u32[]{:S(2)}) copy-start(f32[64]{0:T(128)} %param.16) | copy-start | bytes 772
  0.7 1.0 %copy-start.8 = (f32[128]{0:T(128)S(1)}, f32[128]{0:T(128)}, u32[]{:S(2)}) copy-start(f32[128]{0:T(128)} %param.18) | copy-start | bytes 1540
  1.7 1.0 %copy-start = (bf16[32,32,256]{2,1,0:T(8,128)(2,1)S(1)}, bf16[32,32,256]{2,1,0:T(8,128)(2,1)}, u32[]{:S(2)}) copy-start(bf16[32,32,256]{2,1,0:T(8,128)(2,1)} %param.10) | copy-start | bytes 1572868
  2.7 0.9 %copy-start.1 = (bf16[1024,128]{1,0:T(8,128)(2,1)S(1)}, bf16[1024,128]{1,0:T(8,128)(2,1)}, u32[]{:S(2)}) copy-start(bf16[1024,128]{1,0:T(8,128)(2,1)} %refs_7_.1) | copy-start | bytes 786436
  3.7 0.9 %copy-start.2 = (bf16[32,32,128]{2,1,0:T(8,128)(2,1)S(1)}, bf16[32,32,128]{2,1,0:T(8,128)(2,1)}, u32[]{:S(2)}) copy-start(bf16[32,32,128]{2,1,0:T(8,128)(2,1)} %param.19) | copy-start | bytes 786436

commit v2 on v1

--- a/solution.py
+++ b/solution.py
@@ -10,6 +10,7 @@
 EPSILON = 1e-05
 LANES = 128
 WIDE = 256
+UNROLL = 4
 MESH = pl.DeviceIdType.MESH
 F32 = jnp.float32
 BF16 = jnp.bfloat16
@@ -60,14 +61,19 @@
 
 def fused_kernel(dims, *refs):
     rows, cols, seq_local, res_local, hidden, channels, width = dims
-    (x_hbm, seq_ref, res_ref, gain_ref, shift_ref, w_ref, pb_ref, ow_hbm, ob_ref, cot_hbm) = refs[:10]
-    (pair_hbm, ag_hbm, gw_ref, gpw_ref, vec_ref) = refs[10:15]
+    inputs = refs[:10]
+    (pair_ref, ag_ref, gw_ref, gpw_ref, vec_ref) = refs[10:15]
     (
         x_ref,
+        seq_ref,
+        res_ref,
+        gain_ref,
+        shift_ref,
+        w_ref,
+        pb_ref,
         ow_ref,
+        ob_ref,
         cot_ref,
-        pair_ref,
-        ag_ref,
         scaled_ref,
         inv_ref,
         normed_ref,
@@ -97,18 +103,15 @@
         low_ref,
         sw_ref,
         swr_ref,
-        swc_ref,
-        swcr_ref,
+        swf_ref,
         sv_ref,
         svr_ref,
         svc_ref,
         svcr_ref,
         local_sems,
         one_sems,
-        col_send,
-        col_recv,
-        row_send,
-        row_recv,
+        send_sems,
+        recv_sems,
     ) = refs[15:]
     r = lax.axis_index("row")
     c = lax.axis_index("col")
@@ -134,13 +137,18 @@
         )
         return carry
 
+    staged = (x_ref, seq_ref, res_ref, gain_ref, shift_ref, w_ref, pb_ref, ow_ref, ob_ref, cot_ref)
+    loads = [
+        pltpu.make_async_copy(source, target, local_sems.at[2 + k])
+        for k, (source, target) in enumerate(zip(inputs, staged))
+    ]
+    late = (7, 8, 9)
+    for k, load in enumerate(loads):
+        if k not in late:
+            load.start()
+    for k in late:
+        loads[k].start()
     lax.fori_loop(1, total, greet, 0)
-    load_x = pltpu.make_async_copy(x_hbm, x_ref, local_sems.at[0])
-    load_w = pltpu.make_async_copy(ow_hbm, ow_ref, local_sems.at[1])
-    load_c = pltpu.make_async_copy(cot_hbm, cot_ref, local_sems.at[2])
-    load_x.start()
-    load_w.start()
-    load_c.start()
 
     def remote(src, dst, send_sem, recv_sem, trow, tcol):
         return pltpu.make_async_remote_copy(
@@ -152,40 +160,51 @@
             device_id_type=MESH,
         )
 
-    def over(kind, plane):
+    def over(kind):
         if kind == "col":
-            return cols, c, col_send.at[plane], col_recv.at[plane], lambda k: (r, k)
-        return rows, r, row_send.at[plane], row_recv.at[plane], lambda k: (k, c)
-
-    def start(kind, plane, src, dst):
-        count, me, send, recv, where = over(kind, plane)
+            return cols, c, lambda k: (r, k)
+        if kind == "row":
+            return rows, r, lambda k: (k, c)
+        return total, r * cols + c, lambda k: (k // cols, lax.rem(k, cols))
+
+    def send_to(args, k):
+        kind, plane, src, dst, bulk = args
+        _, me, where = over(kind)
+        remote(src(k), dst(me), send_sems.at[plane], recv_sems.at[plane], *where(k)).start()
+
+    def start(*args):
+        kind = args[0]
+        count, me, _ = over(kind)
 
         def body(t, carry):
-            k = lax.rem(me + t, count)
-            remote(src(k), dst(me), send.at[k], recv.at[me], *where(k)).start()
+            if kind != "row":
+                send_to(args, lax.rem(me + t, count))
+            else:
+                @pl.when(me + t < count)
+                def _():
+                    send_to(args, lax.rem(me + t, count))
+
+                @pl.when(me >= t)
+                def _():
+                    send_to(args, lax.rem(me - t + count, count))
+
             return carry
 
         lax.fori_loop(1, count, body, 0)
 
-    def receive(kind, plane, src, dst):
-        count, me, send, recv, where = over(kind, plane)
-
-        def body(t, carry):
-            k = lax.rem(me + t, count)
-            remote(dst(k), dst(k), send.at[k], recv.at[k], *where(k)).wait_recv()
-            return carry
-
-        lax.fori_loop(1, count, body, 0)
-
-    def drain(kind, plane, src, dst):
-        count, me, send, recv, where = over(kind, plane)
-
-        def body(t, carry):
-            k = lax.rem(me + t, count)
-            remote(src(k), dst(me), send.at[k], recv.at[me], *where(k)).wait_send()
-            return carry
-
-        lax.fori_loop(1, count, body, 0)
+    def everything(kind, plane, bulk):
+        count, me, where = over(kind)
+        part = bulk.at[pl.ds(0, count - 1)]
+        return remote(part, part, send_sems.at[plane], recv_sems.at[plane], *where(lax.rem(me + 1, count)))
+
+    def receive(kind, plane, src, dst, bulk):
+        everything(kind, plane, bulk).wait_recv()
+
+    def drain(kind, plane, src, dst, bulk):
+        everything(kind, plane, bulk).wait_send()
+
+    for k in range(1, 7):
+        loads[k].wait()
 
     def column(mask_ref, count, offset):
         size = mask_ref.shape[1]
@@ -206,15 +225,15 @@
         return jnp.concatenate(parts, axis=0)
 
     w = w_ref[...].astype(F32)
-    w = jnp.concatenate([w, jnp.zeros((channels, LANES - 2 * hidden), F32)], axis=1)
-    w_wide = w.astype(BF16)
-    w_turned = w.T.astype(BF16)
+    w = jnp.concatenate([w, jnp.zeros((LANES - 2 * hidden, channels), F32)], axis=0)
+    w_wide = w.T.astype(BF16)
+    w_turned = w.astype(BF16)
     bias = pb_ref[...]
     bias = jnp.concatenate([bias, jnp.zeros((1, LANES - 2 * hidden), F32)], axis=1)
     gain = gain_ref[...]
     shift = shift_ref[...]
 
-    load_x.wait()
+    loads[0].wait()
 
     def layer_norm(k, carry):
         here = aligned(k * LANES, LANES)
@@ -231,7 +250,7 @@
         tr_ref[here, :] = prj.T
         return carry
 
-    lax.fori_loop(0, chunks, layer_norm, 0)
+    lax.fori_loop(0, chunks, layer_norm, 0, unroll=UNROLL)
 
     for im in range(majors):
         pieces = [prj_ref[pl.ds(im * fold + k, seq_local, stride=res_local), :] for k in range(fold)]
@@ -261,7 +280,7 @@
     left_out = remote(
         lsend_ref, left_slot(relay_col), one_sems.at[0], one_sems.at[1], relay_row, relay_col
     )
-    left_home = pltpu.make_async_copy(lsend_ref, left_slot(c), local_sems.at[3])
+    left_home = pltpu.make_async_copy(lsend_ref, left_slot(c), local_sems.at[0])
 
     @pl.when(at_home)
     def _():
@@ -274,11 +293,11 @@
     def right_block(k):
         return rbuf_ref.at[aligned(k * seq_local, seq_local), :]
 
-    right_args = ("row", 0, lambda k: right_block(r), right_block)
+    right_args = ("row", 0, lambda k: right_block(r), right_block, grr_ref)
+
     start(*right_args)
-
-    load_w.wait()
-    load_c.wait()
+    for k in late:
+        loads[k].wait()
     owf_ref[...] = ow_ref[...].astype(F32)
     for d in range(hidden):
         wp_ref[d * hidden : (d + 1) * hidden, :] = owf_ref[pl.ds(d, hidden, stride=hidden), :].astype(BF16)
@@ -307,7 +326,7 @@
         return carry
 
     steps = pairs // WIDE
-    lax.fori_loop(0, steps // 2, grad_products, 0)
+    lax.fori_loop(0, steps, grad_products, 0)
 
     @pl.when(at_home)
     def _():
@@ -319,33 +338,43 @@
             left_slot(c), left_slot(c), one_sems.at[0], one_sems.at[1], relay_row, relay_col
         ).wait_recv()
 
-    left_args = ("col", 0, lambda k: left_slot(c), left_slot)
+    left_args = ("col", 1, lambda k: left_slot(c), left_slot, glr_ref)
     start(*left_args)
-    lax.fori_loop(steps // 2, steps, grad_products, 0)
-    receive(*right_args)
     receive(*left_args)
-
-    def gl_part(k):
-        return gls_ref.at[aligned((k // factor) * seq_local, seq_local), aligned(lax.rem(k, factor) * block, block)]
-
-    for k in range(tile_rows * hidden // WIDE):
-        gls_ref[:, k * WIDE : (k + 1) * WIDE] = nt(rbuf_ref[...], gp_ref[k * WIDE : (k + 1) * WIDE, :]).astype(BF16)
-    gl_args = ("col", 1, gl_part, lambda k: glr_ref.at[k])
-    start(*gl_args)
     for k in range(block // WIDE):
         grs_ref[:, k * WIDE : (k + 1) * WIDE] = nn(lbuf_ref[...], gp_ref[:, k * WIDE : (k + 1) * WIDE]).astype(BF16)
     gr_args = (
         "row",
-        1,
+        3,
         lambda k: grs_ref.at[aligned(k * seq_local, seq_local), :],
         lambda k: grr_ref.at[k],
+        grr_ref,
     )
+    receive(*right_args)
     start(*gr_args)
 
-    def products(im, carry):
-        left = lbuf_ref[:, aligned(im * LANES, LANES)]
-        for k in range(block // WIDE):
-            tile = tn(left, rbuf_ref[:, k * WIDE : (k + 1) * WIDE])
+    def gl_part(k):
+        return gls_ref.at[aligned((k // factor) * seq_local, seq_local), aligned(lax.rem(k, factor) * block, block)]
+
+    for k in range(tile_rows * hidden // WIDE):
+        gls_ref[:, k * WIDE : (k + 1) * WIDE] = nt(rbuf_ref[...], gp_ref[k * WIDE : (k + 1) * WIDE, :]).astype(BF16)
+    gl_args = ("col", 2, gl_part, lambda k: glr_ref.at[k], glr_ref)
+    start(*gl_args)
+
+    w_block = hidden * hidden // cols
+    gw_row_args = (
+        "col",
+        4,
+        lambda k: gws_ref.at[aligned(k * w_block, w_block), :],
+        lambda k: gwr_ref.at[k],
+        gwr_ref,
+    )
+    for k in range(hidden * hidden // WIDE):
+        rows_here = slice(k * WIDE, (k + 1) * WIDE)
+        right = rbuf_ref[:, k * (WIDE // hidden) * res_local : (k + 1) * (WIDE // hidden) * res_local]
+
+        def products(im, carry, k=k, right=right):
+            tile = tn(lbuf_ref[:, aligned(im * LANES, LANES)], right)
             for h in range(half):
                 blocks = [
                     tile[a * hidden : (a + 1) * hidden, h * LANES : (h + 1) * LANES] for a in range(fold)
@@ -353,10 +382,15 @@
                 for a, swapped in enumerate(lane_group_swap(blocks, res_local)):
                     at = ((k * half + h) * fold + a) * hidden
                     prod_ref[at : at + hidden, aligned(im * LANES, LANES)] = swapped.astype(BF16)
-        return carry
-
-    steps = tile_rows // fold
-    lax.fori_loop(0, steps // 2, products, 0)
+            return carry
+
+        lax.fori_loop(0, tile_rows // fold, products, 0, unroll=8)
+        gws_ref[rows_here, :] = nn(prod_ref[rows_here, :], gpre_ref[...]).astype(BF16)
+        for target in range(k * WIDE // w_block, (k + 1) * WIDE // w_block):
+
+            @pl.when(c != target)
+            def _(target=target):
+                send_to(gw_row_args, target)
 
     receive(*gl_args)
     mine = gls_ref[aligned((c // factor) * seq_local, seq_local), aligned(lax.rem(c, factor) * block, block)]
@@ -366,7 +400,7 @@
 
     glmid_ref[...] = lax.fori_loop(1, cols, add_left, mine.astype(F32)).astype(BF16)
     gl_out = remote(glmid_ref, glfin_ref, one_sems.at[2], one_sems.at[3], relay_row, relay_col)
-    gl_home = pltpu.make_async_copy(glmid_ref, glfin_ref, local_sems.at[4])
+    gl_home = pltpu.make_async_copy(glmid_ref, glfin_ref, local_sems.at[1])
 
     @pl.when(at_home)
     def _():
@@ -375,21 +409,6 @@
     @pl.when(jnp.logical_not(at_home))
     def _():
         gl_out.start()
-
-    lax.fori_loop(steps // 2, steps, products, 0)
-
-    for k in range(hidden * hidden // WIDE):
-        owf_ref[k * WIDE : (k + 1) * WIDE, :] = nn(prod_ref[k * WIDE : (k + 1) * WIDE, :], gpre_ref[...])
-    for k in range(hidden):
-        gws_ref[k * hidden : (k + 1) * hidden, :] = owf_ref[pl.ds(k, hidden, stride=hidden), :].astype(BF16)
-    w_block = hidden * hidden // cols
-    gw_row_args = (
-        "col",
-        2,
-        lambda k: gws_ref.at[aligned(k * w_block, w_block), :],
-        lambda k: gwr_ref.at[k],
-    )
-    start(*gw_row_args)
 
     out_bias = ob_ref[...]
     for k in range(pairs // WIDE):
@@ -399,8 +418,6 @@
             pair_ref[i * res_local : (i + 1) * res_local, :] = (
                 pre[q * res_local : (q + 1) * res_local, :] * inverse_divisor(i)
             ).astype(BF16)
-    store_pair = pltpu.make_async_copy(pair_ref, pair_hbm, local_sems.at[5])
-    store_pair.start()
 
     w_small = w_block // rows
     receive(*gw_row_args)
@@ -412,7 +429,7 @@
     summed = lax.fori_loop(1, cols, add_w, summed).astype(BF16)
     for k in range(rows):
         gwc_ref[k] = summed[k * w_small : (k + 1) * w_small, :]
-    gw_col_args = ("row", 2, lambda k: gwc_ref.at[k], lambda k: gwcr_ref.at[k])
+    gw_col_args = ("row", 5, lambda k: gwc_ref.at[k], lambda k: gwcr_ref.at[k], gwcr_ref)
     start(*gw_col_args)
 
     receive(*gr_args)
@@ -464,68 +481,62 @@
         ag_ref[here, :] = (inv_ref[here, :] * (grad_scaled - first - scaled * second)).astype(BF16)
         return bias_sum, gain_sum, shift_sum
 
+    sums = (jnp.zeros((1, LANES), F32), jnp.zeros((1, channels), F32), jnp.zeros((1, channels), F32))
+    split = chunks // 2
+    sums = lax.fori_loop(0, split, backward, sums, unroll=min(UNROLL, split))
+    receive(*gw_col_args)
+
+    def add_w_col(t, carry):
+        return carry + gwcr_ref[lax.rem(r + t, rows)].astype(F32)
+
+    gwg_ref[r] = lax.fori_loop(1, rows, add_w_col, gwc_ref[r].astype(F32)).astype(BF16)
+    gw_up_args = ("row", 9, lambda k: gwg_ref.at[r], lambda k: gwg_ref.at[k], gwcr_ref)
+    start(*gw_up_args)
+
     bias_sum, gain_sum, shift_sum = lax.fori_loop(
-        0,
-        chunks,
-        backward,
-        (jnp.zeros((1, LANES), F32), jnp.zeros((1, channels), F32), jnp.zeros((1, channels), F32)),
+        split, chunks, backward, sums, unroll=min(UNROLL, chunks - split)
     )
-    store_ag = pltpu.make_async_copy(ag_ref, ag_hbm, local_sems.at[6])
-    store_ag.start()
-    sw_ref[...] = tn(low_ref[...], normed_ref[...])[: 2 * hidden, :].astype(BF16)
+    grad_w_in = tn(low_ref[...], normed_ref[...])
+    quarter = 2 * hidden // cols
+    for k in range(cols):
+        sw_ref[k] = grad_w_in[k * quarter : (k + 1) * quarter, :].astype(BF16)
     sv_ref[0:1, :] = gain_sum
     sv_ref[1:2, :] = shift_sum
     sv_ref[2:3, :] = jnp.concatenate([bias_sum, jnp.zeros((1, channels - LANES), F32)], axis=1)
     sv_ref[3:8, :] = jnp.zeros((5, channels), F32)
-    sw_row_args = ("col", 3, lambda k: sw_ref, lambda k: swr_ref.at[k])
-    sv_row_args = ("col", 4, lambda k: sv_ref, lambda k: svr_ref.at[k])
-    start(*sw_row_args)
+    sw_args = ("all", 6, lambda k: sw_ref.at[lax.rem(k, cols)], lambda k: swr_ref.at[k], swr_ref)
+    sv_row_args = ("col", 7, lambda k: sv_ref, lambda k: svr_ref.at[k], svr_ref)
     start(*sv_row_args)
-
-    receive(*gw_col_args)
-
-    def add_w_col(t, carry):
-        return carry + gwcr_ref[lax.rem(r + t, rows)].astype(F32)
-
-    gwg_ref[r] = lax.fori_loop(1, rows, add_w_col, gwc_ref[r].astype(F32)).astype(BF16)
-    gw_up_args = ("row", 3, lambda k: gwg_ref.at[r], lambda k: gwg_ref.at[k])
-    start(*gw_up_args)
-
-    receive(*sw_row_args)
+    start(*sw_args)
+
+    def ordered(received, count):
+        def add(t, carry):
+            return carry + received[t].astype(F32)
+
+        return lax.fori_loop(1, count, add, received[0].astype(F32))
+
+    svr_ref[c] = sv_ref[...]
     receive(*sv_row_args)
-
-    def add_sw(t, carry):
-        return carry + swr_ref[lax.rem(c + t, cols)].astype(F32)
-
-    def add_sv(t, carry):
-        return carry + svr_ref[lax.rem(c + t, cols)]
-
-    swc_ref[...] = lax.fori_loop(1, cols, add_sw, sw_ref[...].astype(F32)).astype(BF16)
-    svc_ref[...] = lax.fori_loop(1, cols, add_sv, sv_ref[...])
-    sw_col_args = ("row", 4, lambda k: swc_ref, lambda k: swcr_ref.at[k])
-    sv_col_args = ("row", 5, lambda k: svc_ref, lambda k: svcr_ref.at[k])
-    start(*sw_col_args)
+    svc_ref[...] = ordered(svr_ref, cols)
+    sv_col_args = ("row", 8, lambda k: svc_ref, lambda k: svcr_ref.at[k], svcr_ref)
     start(*sv_col_args)
 
     receive(*gw_up_args)
     gw_ref[c] = gwg_ref[...]
-    gw_out_args = ("col", 5, lambda k: gwg_ref, lambda k: gw_ref.at[k])
+    gw_out_args = ("col", 10, lambda k: gwg_ref, lambda k: gw_ref.at[k], gw_ref)
     start(*gw_out_args)
 
-    receive(*sw_col_args)
+    swr_ref[r * cols + c] = sw_ref[c]
+    receive(*sw_args)
+    swf_ref[...] = ordered(swr_ref, total)
+    gpw_ref[c] = swf_ref[...]
+    sw_out_args = ("col", 11, lambda k: swf_ref, lambda k: gpw_ref.at[k], gpw_ref)
+    start(*sw_out_args)
+    svcr_ref[r] = svc_ref[...]
     receive(*sv_col_args)
-
-    def add_swc(t, carry):
-        return carry + swcr_ref[t].astype(F32)
-
-    def add_svc(t, carry):
-        return carry + svcr_ref[t]
-
-    swcr_ref[r] = swc_ref[...]
-    svcr_ref[r] = svc_ref[...]
-    gpw_ref[...] = lax.fori_loop(0, rows, add_swc, jnp.zeros(gpw_ref.shape, F32))
-    vec_ref[...] = lax.fori_loop(0, rows, add_svc, jnp.zeros(vec_ref.shape, F32))
+    vec_ref[...] = ordered(svcr_ref, rows)
     receive(*gw_out_args)
+    receive(*sw_out_args)
 
     @pl.when(jnp.logical_not(at_home))
     def _():
@@ -539,16 +550,35 @@
         gr_args,
         gw_row_args,
         gw_col_args,
-        sw_row_args,
+        sw_args,
         sv_row_args,
         gw_up_args,
-        sw_col_args,
         sv_col_args,
         gw_out_args,
+        sw_out_args,
     ):
         drain(*args)
-    store_pair.wait()
-    store_ag.wait()
+
+
+def finish_kernel(pair_ref, ag_ref, gw_ref, gpw_ref, vec_ref, pair_hbm, ag_hbm, gain_ref, shift_ref, gpw_out, bias_ref, gw_hbm, gwf_ref, mixed_ref, sems):
+    copies = [
+        pltpu.make_async_copy(ag_ref, ag_hbm, sems.at[0]),
+        pltpu.make_async_copy(pair_ref, pair_hbm, sems.at[1]),
+        pltpu.make_async_copy(gwf_ref, gw_hbm, sems.at[2]),
+    ]
+    copies[0].start()
+    copies[1].start()
+    mixed_ref[...] = gw_ref[...].astype(F32)
+    hidden = bias_ref.shape[1] // 2
+    for k in range(hidden):
+        gwf_ref[k * hidden : (k + 1) * hidden, :] = mixed_ref[pl.ds(k, hidden, stride=hidden), :]
+    copies[2].start()
+    gain_ref[...] = vec_ref[0:1, :]
+    shift_ref[...] = vec_ref[1:2, :]
+    bias_ref[...] = vec_ref[2:3, : bias_ref.shape[1]]
+    gpw_out[...] = gpw_ref[...]
+    for copy in copies:
+        copy.wait()
 
 
 def shards(
@@ -578,26 +608,36 @@
     inner = tile_rows * hidden
     w_block = hidden * hidden // cols
     w_small = w_block // rows
+    quarter = 2 * hidden // cols
     dims = (rows, cols, seq_local, res_local, hidden, channels, width)
     vmem = pl.BlockSpec(memory_space=pltpu.VMEM)
-    anywhere = pl.BlockSpec(memory_space=pl.ANY)
+    hbm = pl.BlockSpec(memory_space=pltpu.HBM)
+    operands = [
+        alignment.reshape(n, channels),
+        sequence_mask.reshape(1, -1),
+        residue_mask.reshape(1, -1),
+        layer_norm_gain.reshape(1, -1),
+        norm_shift.reshape(1, -1),
+        proj_weight.T,
+        proj_bias.reshape(1, -1),
+        out_weight,
+        out_bias.reshape(1, -1),
+        cotangent.reshape(pairs, width),
+    ]
+    operands = [pltpu.with_memory_space_constraint(array, pltpu.HBM) for array in operands]
     pair, grad_alignment, grad_w, grad_pw, vectors = pl.pallas_call(
         functools.partial(fused_kernel, dims),
         out_shape=[
             jax.ShapeDtypeStruct((pairs, width), BF16),
             jax.ShapeDtypeStruct((n, channels), BF16),
             jax.ShapeDtypeStruct((cols, rows, w_small, width), BF16),
-            jax.ShapeDtypeStruct((2 * hidden, channels), F32),
+            jax.ShapeDtypeStruct((cols, quarter, channels), F32),
             jax.ShapeDtypeStruct((8, channels), F32),
         ],
-        in_specs=[anywhere, vmem, vmem, vmem, vmem, vmem, vmem, anywhere, vmem, anywhere],
-        out_specs=[anywhere, anywhere, vmem, vmem, vmem],
+        in_specs=[hbm] * 10,
+        out_specs=[vmem] * 5,
         scratch_shapes=[
-            pltpu.VMEM((n, channels), BF16),
-            pltpu.VMEM((hidden * hidden, width), BF16),
-            pltpu.VMEM((pairs, width), BF16),
-            pltpu.VMEM((pairs, width), BF16),
-            pltpu.VMEM((n, channels), BF16),
+            *[pltpu.VMEM(array.shape, array.dtype) for array in operands],
             pltpu.VMEM((n, channels), F32),
             pltpu.VMEM((n, 1), F32),
             pltpu.VMEM((n, channels), BF16),
@@ -625,44 +665,50 @@
             pltpu.VMEM((rows, w_small, width), BF16),
             pltpu.VMEM((rows, w_small, width), BF16),
             pltpu.VMEM((n, LANES), BF16),
-            pltpu.VMEM((2 * hidden, channels), BF16),
-            pltpu.VMEM((cols, 2 * hidden, channels), BF16),
-            pltpu.VMEM((2 * hidden, channels), BF16),
-            pltpu.VMEM((rows, 2 * hidden, channels), BF16),
+            pltpu.VMEM((cols, quarter, channels), BF16),
+            pltpu.VMEM((rows * cols, quarter, channels), BF16),
+            pltpu.VMEM((quarter, channels), F32),
             pltpu.VMEM((8, channels), F32),
             pltpu.VMEM((cols, 8, channels), F32),
             pltpu.VMEM((8, channels), F32),
             pltpu.VMEM((rows, 8, channels), F32),
-            pltpu.SemaphoreType.DMA((7,)),
+            pltpu.SemaphoreType.DMA((12,)),
             pltpu.SemaphoreType.DMA((4,)),
-            pltpu.SemaphoreType.DMA((6, cols)),
-            pltpu.SemaphoreType.DMA((6, cols)),
-            pltpu.SemaphoreType.DMA((6, rows)),
-            pltpu.SemaphoreType.DMA((6, rows)),
+            pltpu.SemaphoreType.DMA((12,)),
+            pltpu.SemaphoreType.DMA((12,)),
         ],
         compiler_params=pltpu.CompilerParams(
             collective_id=0, has_side_effects=True, vmem_limit_bytes=48 * 1024 * 1024
         ),
-    )(
-        alignment.reshape(n, channels),
-        sequence_mask.reshape(1, -1),
-        residue_mask.reshape(1, -1),
-        layer_norm_gain.reshape(1, -1),
-        norm_shift.reshape(1, -1),
-        proj_weight,
-        proj_bias.reshape(1, -1),
-        out_weight,
-        out_bias.reshape(1, -1),
-        cotangent.reshape(pairs, width),
-    )
+    )(*operands)
+    pair, grad_alignment, gain, shift, grad_pw, bias, grad_w = pl.pallas_call(
+        finish_kernel,
+        out_shape=[
+            jax.ShapeDtypeStruct((pairs, width), BF16),
+            jax.ShapeDtypeStruct((n, channels), BF16),
+            jax.ShapeDtypeStruct((1, channels), F32),
+            jax.ShapeDtypeStruct((1, channels), F32),
+            jax.ShapeDtypeStruct((2 * hidden, channels), F32),
+            jax.ShapeDtypeStruct((1, 2 * hidden), F32),
+            jax.ShapeDtypeStruct((hidden * hidden, width), F32),
+        ],
+        in_specs=[vmem] * 5,
+        out_specs=[hbm, hbm, vmem, vmem, vmem, vmem, hbm],
+        scratch_shapes=[
+            pltpu.VMEM((hidden * hidden, width), F32),
+            pltpu.VMEM((hidden * hidden, width), F32),
+            pltpu.SemaphoreType.DMA((3,)),
+        ],
+        compiler_params=pltpu.CompilerParams(vmem_limit_bytes=16 * 1024 * 1024),
+    )(pair, grad_alignment, grad_w.reshape(hidden * hidden, width), grad_pw.reshape(-1, channels), vectors)
     return (
         pair.reshape(tile_rows, res_local, width),
         grad_alignment.reshape(seq_local, res_local, channels),
-        vectors[0],
-        vectors[1],
+        gain.reshape(-1),
+        shift.reshape(-1),
         grad_pw.T,
-        vectors[2, : 2 * hidden],
-        grad_w.reshape(hidden * hidden, width).astype(F32),
+        bias.reshape(-1),
+        grad_w,
     )
 
 

time: 54.2 us -> 41 us (0.76)
  local copies, waits for them, and re-layouts: 7.07 us -> 0 us
  Pallas kernels: 44.9 us -> 40.2 us
  other arithmetic: 0.84 us -> 0 us
    pallas_call x1, Pallas kernels: 44.9 us -> 38.4 us  [shards(): pl.pallas_call(functools.partial(fused_kernel, dims), out_shape=[jax.Shap...]
    unnamed x22 -> x0, local copies, waits for them, and re-layouts: 5.99 us -> none
    pallas_call x0 -> x1, Pallas kernels: none -> 1.81 us  [shards(): pl.pallas_call(finish_kernel, out_shape=[jax.ShapeDtypeStruct((pairs, wid...]
    convert_element_type x1 -> x0, other arithmetic: 0.84 us -> none  [shards(): grad_w.reshape(hidden * hidden, width).astype(F32)]
    slice x1 -> x0, local copies, waits for them, and re-layouts: 0.57 us -> none  [shards(): vectors[1]]
where the time goes in v2:
time: 41 us; the launch traced here: 40.9 us
  Pallas kernels  40.2 us (98%)
  between operations  0.64 us (2%)
    pallas_call x1, Pallas kernels, shards(): pl.pallas_call(functools.partial(fused_kernel, dims), out_shape=[jax.Shap...  38.4 us
    pallas_call x1, Pallas kernels, shards(): pl.pallas_call(finish_kernel, out_shape=[jax.ShapeDtypeStruct((pairs, wid...  1.81 us

profile of v2, /device:TPU:0, one launch (start us, length us, event | category | flops | bytes accessed | tf_op | source)
XLA Modules:
  0.0 40.9 jit_solution(9485861810342187331)
XLA Ops:
  0.6 38.4 %shard_map.153 = (bf16[1024,128]{1,0:T(8,128)(2,1)S(1)}, bf16[1024,256]{1,0:T(8,128)(2,1)S(1)}, bf16[4,4,64,128]{3,2,1,0:T(8,128)(2,1)S(1)}, f32[4,16,256]{2,1,0:T(8,128)S(1)}, f32[8,256]{1,0:T(8,128)S(1)}) custom-call(bf16[1024,256]{1,0:T(8,128)(2,1)} %bitcast.19, s32[1,128]{1,0:T(1,128)} %bitcast.24, s32[1,128]{1,0:T(1,128)} %bitcast.25, ...), custom_call_target="tpu_custom_call" | custom-call | tf_op jit(solution)/shard_map/pallas_call | solution.py:628
  39.1 1.8 %shard_map.154 = (bf16[1024,128]{1,0:T(8,128)(2,1)}, bf16[1024,256]{1,0:T(8,128)(2,1)}, f32[1,256]{1,0:T(1,128)}, f32[1,256]{1,0:T(1,128)}, f32[64,256]{1,0:T(8,...) custom-call(bf16[1024,128]{1,0:T(8,128)(2,1)S(1)} %get-tuple-element.19.pair_ref, ...), custom_call_target="tpu_custom_call" | custom-call | tf_op jit(solution)/shard_map/pallas_call | solution.py:684

commit v3 on v2

--- a/solution.py
+++ b/solution.py
@@ -62,7 +62,7 @@
 def fused_kernel(dims, *refs):
     rows, cols, seq_local, res_local, hidden, channels, width = dims
     inputs = refs[:10]
-    (pair_ref, ag_ref, gw_ref, gpw_ref, vec_ref) = refs[10:15]
+    (pair_ref, ag_ref, gwf_ref, gpw_ref, vec_ref) = refs[10:15]
     (
         x_ref,
         seq_ref,
@@ -76,32 +76,40 @@
         cot_ref,
         scaled_ref,
         inv_ref,
-        normed_ref,
+        both_ref,
         prj_ref,
         tr_ref,
         u_ref,
         seqcol_ref,
         lsend_ref,
         lbuf_ref,
+        lt_ref,
         rbuf_ref,
         owf_ref,
         wp_ref,
+        wpt_ref,
         gpre_ref,
         gp_ref,
         prod_ref,
         gls_ref,
         glr_ref,
+        glp_ref,
+        glx_ref,
         glmid_ref,
         glfin_ref,
         grs_ref,
         grr_ref,
         gws_ref,
         gwr_ref,
+        gwp_ref,
+        gwx_ref,
         gwc_ref,
         gwcr_ref,
-        gwg_ref,
+        gw_ref,
         low_ref,
         sw_ref,
+        swp_ref,
+        swx_ref,
         swr_ref,
         swf_ref,
         sv_ref,
@@ -112,6 +120,8 @@
         one_sems,
         send_sems,
         recv_sems,
+        left_send,
+        left_recv,
     ) = refs[15:]
     r = lax.axis_index("row")
     c = lax.axis_index("col")
@@ -125,6 +135,10 @@
     chunks = n // LANES
     majors = block // LANES
     total = rows * cols
+    chips = cols // 2
+    chip = c // 2
+    core = lax.rem(c, 2)
+    partner = chip * 2 + 1 - core
     barrier = pltpu.get_barrier_semaphore()
 
     def greet(t, carry):
@@ -160,12 +174,16 @@
             device_id_type=MESH,
         )
 
+    gw_bulk = gws_ref.at[pl.ds(0, (rows * chips - 1) * (hidden * hidden // total)), :]
+
     def over(kind):
         if kind == "col":
             return cols, c, lambda k: (r, k)
         if kind == "row":
             return rows, r, lambda k: (k, c)
-        return total, r * cols + c, lambda k: (k // cols, lax.rem(k, cols))
+        if kind == "chip":
+            return chips, chip, lambda k: (r, 2 * k + core)
+        return rows * chips, r * chips + chip, lambda k: (k // chips, 2 * lax.rem(k, chips) + core)
 
     def send_to(args, k):
         kind, plane, src, dst, bulk = args
@@ -194,8 +212,14 @@
 
     def everything(kind, plane, bulk):
         count, me, where = over(kind)
-        part = bulk.at[pl.ds(0, count - 1)]
+        part = bulk if bulk is gw_bulk else bulk.at[pl.ds(0, count - 1)]
         return remote(part, part, send_sems.at[plane], recv_sems.at[plane], *where(lax.rem(me + 1, count)))
+
+    def hand(plane, src, dst):
+        remote(src, dst, send_sems.at[plane], recv_sems.at[plane], r, partner).start()
+
+    def handed(plane, bulk):
+        return remote(bulk, bulk, send_sems.at[plane], recv_sems.at[plane], r, partner)
 
     def receive(kind, plane, src, dst, bulk):
         everything(kind, plane, bulk).wait_recv()
@@ -244,13 +268,14 @@
         normed = (scaled * gain + shift).astype(BF16)
         scaled_ref[here, :] = scaled
         inv_ref[here, :] = inverse
-        normed_ref[here, :] = normed
+        both_ref[here, :channels] = normed
+        both_ref[here, channels:] = scaled.astype(BF16)
         prj = (nn(normed, w_wide) + bias) * live_column(k)
         prj_ref[here, :] = prj
         tr_ref[here, :] = prj.T
         return carry
 
-    lax.fori_loop(0, chunks, layer_norm, 0, unroll=UNROLL)
+    lax.fori_loop(0, chunks, layer_norm, 0, unroll=min(2 * UNROLL, chunks))
 
     for im in range(majors):
         pieces = [prj_ref[pl.ds(im * fold + k, seq_local, stride=res_local), :] for k in range(fold)]
@@ -276,19 +301,51 @@
 
     relay_row = c // factor
     relay_col = r * factor + lax.rem(c, factor)
-    at_home = jnp.logical_and(relay_row == r, relay_col == c)
+    left_col = chip * 2 + lax.rem(r, 2)
+    left_stays = jnp.logical_and(relay_row == r, left_col == c)
     left_out = remote(
-        lsend_ref, left_slot(relay_col), one_sems.at[0], one_sems.at[1], relay_row, relay_col
+        lsend_ref, left_slot(relay_col), one_sems.at[0], left_recv.at[relay_col], relay_row, left_col
     )
-    left_home = pltpu.make_async_copy(lsend_ref, left_slot(c), local_sems.at[0])
-
-    @pl.when(at_home)
+    left_home = pltpu.make_async_copy(lsend_ref, left_slot(relay_col), local_sems.at[0])
+
+    @pl.when(left_stays)
     def _():
         left_home.start()
 
-    @pl.when(jnp.logical_not(at_home))
+    @pl.when(jnp.logical_not(left_stays))
     def _():
         left_out.start()
+
+    HAND_GL, HAND_A, HAND_B, HAND_LEFT, HAND_OUT, HAND_SW = 12, 13, 14, 15, 16, 10
+
+    def passed(i, q):
+        row = 2 * lax.rem(r // 2 + i, rows // 2) + core
+        near = (r * factor + q) // 2 == chip
+        return row * factor + q, near, jnp.logical_and(row == r, r * factor + q == c)
+
+    def pass_left(i):
+        for q in range(factor):
+            k, near, own = passed(i, q)
+            slot = left_slot(k)
+
+            @pl.when(own)
+            def _():
+                left_home.wait()
+
+            @pl.when(jnp.logical_not(own))
+            def _():
+                remote(slot, slot, one_sems.at[0], left_recv.at[k], r, partner).wait_recv()
+
+            @pl.when(near)
+            def _():
+                def body(t, carry):
+                    other = lax.rem(chip + t, chips)
+                    remote(slot, slot, left_send.at[k], left_recv.at[k], r, 2 * other + core).start()
+                    return carry
+
+                lax.fori_loop(1, chips, body, 0)
+
+            hand(HAND_LEFT, slot, slot)
 
     def right_block(k):
         return rbuf_ref.at[aligned(k * seq_local, seq_local), :]
@@ -326,21 +383,13 @@
         return carry
 
     steps = pairs // WIDE
-    lax.fori_loop(0, steps, grad_products, 0)
-
-    @pl.when(at_home)
-    def _():
-        left_home.wait()
-
-    @pl.when(jnp.logical_not(at_home))
-    def _():
-        remote(
-            left_slot(c), left_slot(c), one_sems.at[0], one_sems.at[1], relay_row, relay_col
-        ).wait_recv()
-
-    left_args = ("col", 1, lambda k: left_slot(c), left_slot, glr_ref)
-    start(*left_args)
-    receive(*left_args)
+    lax.fori_loop(0, steps // 2, grad_products, 0)
+    pass_left(0)
+    lax.fori_loop(steps // 2, steps, grad_products, 0)
+
+    for i in range(1, rows // 2):
+        pass_left(i)
+    handed(HAND_LEFT, glp_ref).wait_recv()
     for k in range(block // WIDE):
         grs_ref[:, k * WIDE : (k + 1) * WIDE] = nn(lbuf_ref[...], gp_ref[:, k * WIDE : (k + 1) * WIDE]).astype(BF16)
     gr_args = (
@@ -350,6 +399,10 @@
         lambda k: grr_ref.at[k],
         grr_ref,
     )
+    for im in range(tile_rows * hidden // LANES):
+        lt_ref[im * LANES : (im + 1) * LANES, :] = lbuf_ref[:, im * LANES : (im + 1) * LANES].T
+    for k in range(hidden * hidden // LANES):
+        wpt_ref[:, k * LANES : (k + 1) * LANES] = wp_ref[k * LANES : (k + 1) * LANES, :].T
     receive(*right_args)
     start(*gr_args)
 
@@ -358,48 +411,98 @@
 
     for k in range(tile_rows * hidden // WIDE):
         gls_ref[:, k * WIDE : (k + 1) * WIDE] = nt(rbuf_ref[...], gp_ref[k * WIDE : (k + 1) * WIDE, :]).astype(BF16)
-    gl_args = ("col", 2, gl_part, lambda k: glr_ref.at[k], glr_ref)
-    start(*gl_args)
+
+    def hand_left(k, carry):
+        hand(HAND_GL, gl_part((1 - core) * chips + k), glp_ref.at[k])
+        return carry
+
+    lax.fori_loop(0, chips, hand_left, 0)
+    gl_args = ("chip", 2, lambda k: glx_ref.at[k], lambda k: glr_ref.at[k], glr_ref)
+
+    def sum_left():
+        handed(HAND_GL, glp_ref).wait_recv()
+
+        def add(k, carry):
+            t = core * chips + k
+            mine = gls_ref[aligned((t // factor) * seq_local, seq_local), aligned(lax.rem(t, factor) * block, block)]
+            glx_ref[k] = (mine.astype(F32) + glp_ref[k].astype(F32)).astype(BF16)
+            return carry
+
+        lax.fori_loop(0, chips, add, 0)
+        start(*gl_args)
+
 
     w_block = hidden * hidden // cols
-    gw_row_args = (
-        "col",
-        4,
-        lambda k: gws_ref.at[aligned(k * w_block, w_block), :],
-        lambda k: gwr_ref.at[k],
-        gwr_ref,
-    )
-    for k in range(hidden * hidden // WIDE):
-        rows_here = slice(k * WIDE, (k + 1) * WIDE)
-        right = rbuf_ref[:, k * (WIDE // hidden) * res_local : (k + 1) * (WIDE // hidden) * res_local]
-
-        def products(im, carry, k=k, right=right):
-            tile = tn(lbuf_ref[:, aligned(im * LANES, LANES)], right)
+    gw_row_args = ("chip", 4, lambda k: gwx_ref.at[k], lambda k: gwr_ref.at[k], gwr_ref)
+    strips = hidden * hidden // WIDE
+    per = WIDE // w_block
+    first = lax.rem((chip + 1) * 2 * w_block // WIDE, strips)
+
+    def sum_weight(later):
+        plane = HAND_B if later else HAND_A
+        some = chips // 2
+        offset = some if later else 0
+        handed(plane, gwp_ref.at[pl.ds(0, some)]).wait_recv()
+
+        def add(k, carry):
+            k = lax.rem(first * per // 2 + offset + k, chips)
+            t = 2 * k + core
+            mine = gws_ref[aligned(t * w_block, w_block), :]
+            gwx_ref[k] = (mine.astype(F32) + gwp_ref[k].astype(F32)).astype(BF16)
+
+            @pl.when(k != chip)
+            def _():
+                send_to(gw_row_args, k)
+
+            return carry
+
+        lax.fori_loop(0, some, add, 0)
+
+    for k in range(strips):
+        strip = lax.rem(first + k, strips)
+        right = rbuf_ref[:, aligned(strip * WIDE, WIDE)]
+
+        def products(im, carry, strip=strip, right=right):
+            tile = nn(lt_ref[aligned(im * LANES, LANES), :], right)
             for h in range(half):
                 blocks = [
                     tile[a * hidden : (a + 1) * hidden, h * LANES : (h + 1) * LANES] for a in range(fold)
                 ]
                 for a, swapped in enumerate(lane_group_swap(blocks, res_local)):
-                    at = ((k * half + h) * fold + a) * hidden
-                    prod_ref[at : at + hidden, aligned(im * LANES, LANES)] = swapped.astype(BF16)
+                    at = strip * WIDE + (h * fold + a) * hidden
+                    prod_ref[aligned(at, hidden), aligned(im * LANES, LANES)] = swapped.astype(BF16)
             return carry
 
         lax.fori_loop(0, tile_rows // fold, products, 0, unroll=8)
-        gws_ref[rows_here, :] = nn(prod_ref[rows_here, :], gpre_ref[...]).astype(BF16)
-        for target in range(k * WIDE // w_block, (k + 1) * WIDE // w_block):
-
-            @pl.when(c != target)
-            def _(target=target):
-                send_to(gw_row_args, target)
+        here = aligned(strip * WIDE, WIDE)
+        gws_ref[here, :] = nn(prod_ref[here, :], gpre_ref[...]).astype(BF16)
+        for j in range(per):
+            target = strip * per + j
+
+            @pl.when(lax.rem(target, 2) != core)
+            def _(target=target, k=k):
+                hand(
+                    HAND_A if k < strips // 2 else HAND_B,
+                    gws_ref.at[aligned(target * w_block, w_block), :],
+                    gwp_ref.at[target // 2],
+                )
+
+        if k == 0:
+            sum_left()
+        if k == strips // 2:
+            sum_weight(False)
 
     receive(*gl_args)
-    mine = gls_ref[aligned((c // factor) * seq_local, seq_local), aligned(lax.rem(c, factor) * block, block)]
 
     def add_left(t, carry):
-        return carry + glr_ref[lax.rem(c + t, cols)].astype(F32)
-
-    glmid_ref[...] = lax.fori_loop(1, cols, add_left, mine.astype(F32)).astype(BF16)
-    gl_out = remote(glmid_ref, glfin_ref, one_sems.at[2], one_sems.at[3], relay_row, relay_col)
+        return carry + glr_ref[lax.rem(chip + t, chips)].astype(F32)
+
+    glmid_ref[...] = lax.fori_loop(1, chips, add_left, glx_ref[chip].astype(F32)).astype(BF16)
+    gathered = core * chips + chip
+    owner_row = gathered // factor
+    owner_col = r * factor + lax.rem(gathered, factor)
+    at_home = jnp.logical_and(owner_row == r, owner_col == c)
+    gl_out = remote(glmid_ref, glfin_ref, one_sems.at[2], one_sems.at[3], owner_row, owner_col)
     gl_home = pltpu.make_async_copy(glmid_ref, glfin_ref, local_sems.at[1])
 
     @pl.when(at_home)
@@ -412,21 +515,21 @@
 
     out_bias = ob_ref[...]
     for k in range(pairs // WIDE):
-        pre = tn(wp_ref[...], prod_ref[:, k * WIDE : (k + 1) * WIDE]).T + out_bias
+        pre = nn(wpt_ref[...], prod_ref[:, k * WIDE : (k + 1) * WIDE]).T + out_bias
         for q in range(WIDE // res_local):
             i = k * (WIDE // res_local) + q
             pair_ref[i * res_local : (i + 1) * res_local, :] = (
                 pre[q * res_local : (q + 1) * res_local, :] * inverse_divisor(i)
             ).astype(BF16)
 
+    sum_weight(True)
     w_small = w_block // rows
     receive(*gw_row_args)
-    summed = gws_ref[aligned(c * w_block, w_block), :].astype(F32)
 
     def add_w(t, carry):
-        return carry + gwr_ref[lax.rem(c + t, cols)].astype(F32)
-
-    summed = lax.fori_loop(1, cols, add_w, summed).astype(BF16)
+        return carry + gwr_ref[lax.rem(chip + t, chips)].astype(F32)
+
+    summed = lax.fori_loop(1, chips, add_w, gwx_ref[chip].astype(F32)).astype(BF16)
     for k in range(rows):
         gwc_ref[k] = summed[k * w_small : (k + 1) * w_small, :]
     gw_col_args = ("row", 5, lambda k: gwc_ref.at[k], lambda k: gwcr_ref.at[k], gwcr_ref)
@@ -447,13 +550,18 @@
             turned = place_groups(pieces, [(q - k) * res_local for q in range(fold)], res_local)
             tr_ref[pl.ds(sb * LANES + hidden + k, majors, stride=fold), :] = turned
 
-    @pl.when(at_home)
+    giver = r * factor + lax.rem(c, factor)
+    giver_row = c // factor
+    giver_col = 2 * lax.rem(giver, chips) + giver // chips
+    kept_here = jnp.logical_and(giver_row == r, giver_col == c)
+
+    @pl.when(kept_here)
     def _():
         gl_home.wait()
 
-    @pl.when(jnp.logical_not(at_home))
+    @pl.when(jnp.logical_not(kept_here))
     def _():
-        remote(glmid_ref, glfin_ref, one_sems.at[2], one_sems.at[3], relay_row, relay_col).wait_recv()
+        remote(glmid_ref, glfin_ref, one_sems.at[2], one_sems.at[3], giver_row, giver_col).wait_recv()
 
     for im in range(majors):
         piece = glfin_ref[:, im * LANES : (im + 1) * LANES].astype(F32)
@@ -463,51 +571,70 @@
 
     lane = lax.broadcasted_iota(jnp.int32, (LANES, LANES), 1)
 
-    def backward(k, carry):
-        bias_sum, gain_sum, shift_sum = carry
+    def lower(k, bias_sum):
         here = aligned(k * LANES, LANES)
         projected = jnp.where(lane < hidden, prj_ref[here, :], tr_ref[here, :].T)
         projected = jnp.where(lane < 2 * hidden, projected * live_column(k), 0.0)
-        low = projected.astype(BF16)
-        low_ref[here, :] = low
-        upstream = nn(low, w_turned)
+        low_ref[here, :] = projected.astype(BF16)
+        return bias_sum + jnp.sum(projected, axis=0, keepdims=True)
+
+    bias_sum = lax.fori_loop(0, chunks, lower, jnp.zeros((1, LANES), F32), unroll=min(2 * UNROLL, chunks))
+    joined = tn(low_ref[...], both_ref[...])
+    grad_w_in = joined[:, :channels]
+    low_sum = jnp.sum(low_ref[...].astype(F32), axis=0, keepdims=True)
+    turned = w_turned.astype(F32)
+    sv_ref[0:1, :] = jnp.sum(joined[:, channels:] * turned, axis=0, keepdims=True)
+    sv_ref[1:2, :] = jnp.sum(low_sum.T * turned, axis=0, keepdims=True)
+    quarter = 2 * hidden // cols
+    for k in range(cols):
+        sw_ref[k] = grad_w_in[k * quarter : (k + 1) * quarter, :].astype(BF16)
+    sv_ref[2:3, :] = jnp.concatenate([bias_sum, jnp.zeros((1, channels - LANES), F32)], axis=1)
+    sv_ref[3:8, :] = jnp.zeros((5, channels), F32)
+    sv_row_args = ("col", 7, lambda k: sv_ref, lambda k: svr_ref.at[k], svr_ref)
+    start(*sv_row_args)
+
+    def hand_sw(k, carry):
+        hand(HAND_SW, sw_ref.at[2 * k + 1 - core], swp_ref.at[k])
+        return carry
+
+    lax.fori_loop(0, chips, hand_sw, 0)
+
+    def backward(k, carry):
+        here = aligned(k * LANES, LANES)
         scaled = scaled_ref[here, :]
-        bias_sum = bias_sum + jnp.sum(projected, axis=0, keepdims=True)
-        gain_sum = gain_sum + jnp.sum(upstream * scaled, axis=0, keepdims=True)
-        shift_sum = shift_sum + jnp.sum(upstream, axis=0, keepdims=True)
-        grad_scaled = upstream * gain
+        grad_scaled = nn(low_ref[here, :], w_turned) * gain
         first = jnp.mean(grad_scaled, axis=-1, keepdims=True)
         second = jnp.mean(grad_scaled * scaled, axis=-1, keepdims=True)
         ag_ref[here, :] = (inv_ref[here, :] * (grad_scaled - first - scaled * second)).astype(BF16)
-        return bias_sum, gain_sum, shift_sum
-
-    sums = (jnp.zeros((1, LANES), F32), jnp.zeros((1, channels), F32), jnp.zeros((1, channels), F32))
+        return carry
+
     split = chunks // 2
-    sums = lax.fori_loop(0, split, backward, sums, unroll=min(UNROLL, split))
+    lax.fori_loop(0, split, backward, 0, unroll=min(UNROLL, split))
+    handed(HAND_SW, swp_ref).wait_recv()
+
+    def add_sw(k, carry):
+        swx_ref[k] = (sw_ref[2 * k + core].astype(F32) + swp_ref[k].astype(F32)).astype(BF16)
+        return carry
+
+    lax.fori_loop(0, chips, add_sw, 0)
+    sw_args = ("core", 6, lambda k: swx_ref.at[lax.rem(k, chips)], lambda k: swr_ref.at[k], swr_ref)
+    start(*sw_args)
     receive(*gw_col_args)
 
     def add_w_col(t, carry):
         return carry + gwcr_ref[lax.rem(r + t, rows)].astype(F32)
 
-    gwg_ref[r] = lax.fori_loop(1, rows, add_w_col, gwc_ref[r].astype(F32)).astype(BF16)
-    gw_up_args = ("row", 9, lambda k: gwg_ref.at[r], lambda k: gwg_ref.at[k], gwcr_ref)
-    start(*gw_up_args)
-
-    bias_sum, gain_sum, shift_sum = lax.fori_loop(
-        split, chunks, backward, sums, unroll=min(UNROLL, chunks - split)
+    gw_ref[c, r] = lax.fori_loop(1, rows, add_w_col, gwc_ref[r].astype(F32)).astype(BF16)
+    gw_all_args = (
+        "core",
+        9,
+        lambda k: gw_ref.at[c, r],
+        lambda k: gw_ref.at[2 * lax.rem(k, chips) + core, k // chips],
+        gw_bulk,
     )
-    grad_w_in = tn(low_ref[...], normed_ref[...])
-    quarter = 2 * hidden // cols
-    for k in range(cols):
-        sw_ref[k] = grad_w_in[k * quarter : (k + 1) * quarter, :].astype(BF16)
-    sv_ref[0:1, :] = gain_sum
-    sv_ref[1:2, :] = shift_sum
-    sv_ref[2:3, :] = jnp.concatenate([bias_sum, jnp.zeros((1, channels - LANES), F32)], axis=1)
-    sv_ref[3:8, :] = jnp.zeros((5, channels), F32)
-    sw_args = ("all", 6, lambda k: sw_ref.at[lax.rem(k, cols)], lambda k: swr_ref.at[k], swr_ref)
-    sv_row_args = ("col", 7, lambda k: sv_ref, lambda k: svr_ref.at[k], svr_ref)
-    start(*sv_row_args)
-    start(*sw_args)
+    start(*gw_all_args)
+
+    lax.fori_loop(split, chunks, backward, 0, unroll=min(UNROLL, chunks - split))
 
     def ordered(received, count):
         def add(t, carry):
@@ -521,58 +648,86 @@
     sv_col_args = ("row", 8, lambda k: svc_ref, lambda k: svcr_ref.at[k], svcr_ref)
     start(*sv_col_args)
 
-    receive(*gw_up_args)
-    gw_ref[c] = gwg_ref[...]
-    gw_out_args = ("col", 10, lambda k: gwg_ref, lambda k: gw_ref.at[k], gw_ref)
-    start(*gw_out_args)
-
-    swr_ref[r * cols + c] = sw_ref[c]
+    receive(*gw_all_args)
+
+    def hand_out(k, carry):
+        slot = gw_ref.at[2 * k + core]
+        hand(HAND_OUT, slot, slot)
+        return carry
+
+    lax.fori_loop(0, chips, hand_out, 0)
+    swr_ref[r * chips + chip] = swx_ref[chip]
     receive(*sw_args)
-    swf_ref[...] = ordered(swr_ref, total)
+    swf_ref[...] = ordered(swr_ref, rows * chips)
     gpw_ref[c] = swf_ref[...]
     sw_out_args = ("col", 11, lambda k: swf_ref, lambda k: gpw_ref.at[k], gpw_ref)
     start(*sw_out_args)
     svcr_ref[r] = svc_ref[...]
     receive(*sv_col_args)
     vec_ref[...] = ordered(svcr_ref, rows)
-    receive(*gw_out_args)
+    handed(HAND_OUT, gw_ref.at[pl.ds(0, chips)]).wait_recv()
+    for t in range(cols):
+        for k in range(rows):
+            at = (t * rows + k) * w_small
+            owf_ref[at : at + w_small, :] = gw_ref[t, k].astype(F32)
+    for k in range(hidden):
+        gwf_ref[k * hidden : (k + 1) * hidden, :] = owf_ref[pl.ds(k, hidden, stride=hidden), :]
     receive(*sw_out_args)
 
     @pl.when(jnp.logical_not(at_home))
     def _():
+        gl_out.wait_send()
+
+    @pl.when(jnp.logical_not(left_stays))
+    def _():
         left_out.wait_send()
-        gl_out.wait_send()
-
+
+    for i in range(rows // 2):
+        for q in range(factor):
+            k, near, _ = passed(i, q)
+
+            @pl.when(near)
+            def _():
+                rest = glr_ref.at[pl.ds(0, chips - 1)]
+                remote(rest, rest, left_send.at[k], left_recv.at[k], r, partner).wait_send()
+
+    handed(HAND_LEFT, glp_ref).wait_send()
+    handed(HAND_SW, swp_ref).wait_send()
+    handed(HAND_GL, glp_ref).wait_send()
+    handed(HAND_OUT, gw_ref.at[pl.ds(0, chips)]).wait_send()
+    for plane in (HAND_A, HAND_B):
+        handed(plane, gwp_ref.at[pl.ds(0, chips // 2)]).wait_send()
     for args in (
         right_args,
-        left_args,
         gl_args,
         gr_args,
         gw_row_args,
         gw_col_args,
         sw_args,
         sv_row_args,
-        gw_up_args,
+        gw_all_args,
         sv_col_args,
-        gw_out_args,
         sw_out_args,
     ):
         drain(*args)
 
 
-def finish_kernel(pair_ref, ag_ref, gw_ref, gpw_ref, vec_ref, pair_hbm, ag_hbm, gain_ref, shift_ref, gpw_out, bias_ref, gw_hbm, gwf_ref, mixed_ref, sems):
-    copies = [
-        pltpu.make_async_copy(ag_ref, ag_hbm, sems.at[0]),
-        pltpu.make_async_copy(pair_ref, pair_hbm, sems.at[1]),
-        pltpu.make_async_copy(gwf_ref, gw_hbm, sems.at[2]),
-    ]
-    copies[0].start()
-    copies[1].start()
-    mixed_ref[...] = gw_ref[...].astype(F32)
-    hidden = bias_ref.shape[1] // 2
-    for k in range(hidden):
-        gwf_ref[k * hidden : (k + 1) * hidden, :] = mixed_ref[pl.ds(k, hidden, stride=hidden), :]
-    copies[2].start()
+def finish_kernel(pair_ref, ag_ref, gw_ref, gpw_ref, vec_ref, pair_hbm, ag_hbm, gain_ref, shift_ref, gpw_out, bias_ref, gw_hbm, sems):
+    copies = []
+
+    def send(source, target, parts, part):
+        size = source.shape[0] // parts
+        here = pl.ds(part * size, size)
+        copy = pltpu.make_async_copy(source.at[here, :], target.at[here, :], sems.at[len(copies)])
+        copy.start()
+        copies.append(copy)
+
+    for part in range(4):
+        send(ag_ref, ag_hbm, 4, part)
+    for part in range(2):
+        send(pair_ref, pair_hbm, 2, part)
+    for part in range(4):
+        send(gw_ref, gw_hbm, 4, part)
     gain_ref[...] = vec_ref[0:1, :]
     shift_ref[...] = vec_ref[1:2, :]
     bias_ref[...] = vec_ref[2:3, : bias_ref.shape[1]]
@@ -630,7 +785,7 @@
         out_shape=[
             jax.ShapeDtypeStruct((pairs, width), BF16),
             jax.ShapeDtypeStruct((n, channels), BF16),
-            jax.ShapeDtypeStruct((cols, rows, w_small, width), BF16),
+            jax.ShapeDtypeStruct((hidden * hidden, width), F32),
             jax.ShapeDtypeStruct((cols, quarter, channels), F32),
             jax.ShapeDtypeStruct((8, channels), F32),
         ],
@@ -640,33 +795,41 @@
             *[pltpu.VMEM(array.shape, array.dtype) for array in operands],
             pltpu.VMEM((n, channels), F32),
             pltpu.VMEM((n, 1), F32),
-            pltpu.VMEM((n, channels), BF16),
+            pltpu.VMEM((n, 2 * channels), BF16),
             pltpu.VMEM((n, LANES), F32),
             pltpu.VMEM((n, LANES), F32),
             pltpu.VMEM((majors * seq_local, LANES), F32),
             pltpu.VMEM((seq_local, LANES), F32),
             pltpu.VMEM((seq_local, block), BF16),
             pltpu.VMEM((seqs, inner), BF16),
+            pltpu.VMEM((inner, seqs), BF16),
             pltpu.VMEM((seqs, block), BF16),
             pltpu.VMEM((hidden * hidden, width), F32),
             pltpu.VMEM((hidden * hidden, width), BF16),
+            pltpu.VMEM((width, hidden * hidden), BF16),
             pltpu.VMEM((pairs, width), BF16),
             pltpu.VMEM((inner, block), BF16),
             pltpu.VMEM((hidden * hidden, pairs), BF16),
             pltpu.VMEM((seqs, inner), BF16),
             pltpu.VMEM((cols, seq_local, block), BF16),
+            pltpu.VMEM((cols // 2, seq_local, block), BF16),
+            pltpu.VMEM((cols // 2, seq_local, block), BF16),
             pltpu.VMEM((seq_local, block), BF16),
             pltpu.VMEM((seq_local, block), BF16),
             pltpu.VMEM((seqs, block), BF16),
             pltpu.VMEM((rows, seq_local, block), BF16),
             pltpu.VMEM((hidden * hidden, width), BF16),
-            pltpu.VMEM((cols, w_block, width), BF16),
+            pltpu.VMEM((cols // 2, w_block, width), BF16),
+            pltpu.VMEM((cols // 2, w_block, width), BF16),
+            pltpu.VMEM((cols // 2, w_block, width), BF16),
             pltpu.VMEM((rows, w_small, width), BF16),
             pltpu.VMEM((rows, w_small, width), BF16),
-            pltpu.VMEM((rows, w_small, width), BF16),
+            pltpu.VMEM((cols, rows, w_small, width), BF16),
             pltpu.VMEM((n, LANES), BF16),
             pltpu.VMEM((cols, quarter, channels), BF16),
-            pltpu.VMEM((rows * cols, quarter, channels), BF16),
+            pltpu.VMEM((cols // 2, quarter, channels), BF16),
+            pltpu.VMEM((cols // 2, quarter, channels), BF16),
+            pltpu.VMEM((rows * cols // 2, quarter, channels), BF16),
             pltpu.VMEM((quarter, channels), F32),
             pltpu.VMEM((8, channels), F32),
             pltpu.VMEM((cols, 8, channels), F32),
@@ -674,8 +837,10 @@
             pltpu.VMEM((rows, 8, channels), F32),
             pltpu.SemaphoreType.DMA((12,)),
             pltpu.SemaphoreType.DMA((4,)),
-            pltpu.SemaphoreType.DMA((12,)),
-            pltpu.SemaphoreType.DMA((12,)),
+            pltpu.SemaphoreType.DMA((17,)),
+            pltpu.SemaphoreType.DMA((17,)),
+            pltpu.SemaphoreType.DMA((cols,)),
+            pltpu.SemaphoreType.DMA((cols,)),
         ],
         compiler_params=pltpu.CompilerParams(
             collective_id=0, has_side_effects=True, vmem_limit_bytes=48 * 1024 * 1024
@@ -695,12 +860,10 @@
         in_specs=[vmem] * 5,
         out_specs=[hbm, hbm, vmem, vmem, vmem, vmem, hbm],
         scratch_shapes=[
-            pltpu.VMEM((hidden * hidden, width), F32),
-            pltpu.VMEM((hidden * hidden, width), F32),
-            pltpu.SemaphoreType.DMA((3,)),
+            pltpu.SemaphoreType.DMA((10,)),
         ],
         compiler_params=pltpu.CompilerParams(vmem_limit_bytes=16 * 1024 * 1024),
-    )(pair, grad_alignment, grad_w.reshape(hidden * hidden, width), grad_pw.reshape(-1, channels), vectors)
+    )(pair, grad_alignment, grad_w, grad_pw.reshape(-1, channels), vectors)
     return (
         pair.reshape(tile_rows, res_local, width),
         grad_alignment.reshape(seq_local, res_local, channels),

time: 41 us -> 39 us (0.951)
  Pallas kernels: 40.2 us -> 38.2 us
    pallas_call x1, Pallas kernels: 38.4 us -> 36.4 us  [shards(): pl.pallas_call(functools.partial(fused_kernel, dims), out_shape=[jax.Shap...]
where the time goes in v3:
time: 39 us; the launch traced here: 38.8 us
  Pallas kernels  38.2 us (98%)
  between operations  0.64 us (2%)
    pallas_call x1, Pallas kernels, shards(): pl.pallas_call(functools.partial(fused_kernel, dims), out_shape=[jax.Shap...  36.4 us
    pallas_call x1, Pallas kernels, shards(): pl.pallas_call(finish_kernel, out_shape=[jax.ShapeDtypeStruct((pairs, wid...  1.77 us

profile of v3, /device:TPU:0, one launch (start us, length us, event | category | flops | bytes accessed | tf_op | source)
XLA Modules:
  0.0 38.8 jit_solution(6771472897985223457)
XLA Ops:
  0.6 36.4 %shard_map.153 = (bf16[1024,128]{1,0:T(8,128)(2,1)S(1)}, bf16[1024,256]{1,0:T(8,128)(2,1)S(1)}, f32[1024,128]{1,0:T(8,128)S(1)}, f32[4,16,256]{2,1,0:T(8,128)S(1)}, f32[8,256]{1,0:T(8,128)S(1)}) custom-call(bf16[1024,256]{1,0:T(8,128)(2,1)} %bitcast.17, s32[1,128]{1,0:T(1,128)} %bitcast.22, s32[1,128]{1,0:T(1,128)} %bitcast.23, f32[1,256]{1,0:T(1,128)} %bitcast.20, ...), custom_call_target="tpu_custom_call" | custom-call | tf_op jit(solution)/shard_map/pallas_call | solution.py:783
  37.0 1.8 %shard_map.154 = (bf16[1024,128]{1,0:T(8,128)(2,1)}, bf16[1024,256]{1,0:T(8,128)(2,1)}, f32[1,256]{1,0:T(1,128)}, f32[1,256]{1,0:T(1,128)}, f32[64,256]{1,0:T(8,...) custom-call(bf16[1024,128]{1,0:T(8,128)(2,1)S(1)} %get-tuple-element.19.pair_ref, ...), custom_call_target="tpu_custom_call" | custom-call | tf_op jit(solution)/shard_map/pallas_call | solution.py:849

commit v4 on v3

--- a/solution.py
+++ b/solution.py
@@ -114,8 +114,8 @@
         swf_ref,
         sv_ref,
         svr_ref,
+        svp_ref,
         svc_ref,
-        svcr_ref,
         local_sems,
         one_sems,
         send_sems,
@@ -157,12 +157,11 @@
         for k, (source, target) in enumerate(zip(inputs, staged))
     ]
     late = (7, 8, 9)
-    for k, load in enumerate(loads):
-        if k not in late:
-            load.start()
+    for load in loads[: late[0]]:
+        load.start()
+    lax.fori_loop(1, total, greet, 0)
     for k in late:
         loads[k].start()
-    lax.fori_loop(1, total, greet, 0)
 
     def remote(src, dst, send_sem, recv_sem, trow, tcol):
         return pltpu.make_async_remote_copy(
@@ -190,7 +189,7 @@
         _, me, where = over(kind)
         remote(src(k), dst(me), send_sems.at[plane], recv_sems.at[plane], *where(k)).start()
 
-    def start(*args):
+    def start(*args, first=1, last=None):
         kind = args[0]
         count, me, _ = over(kind)
 
@@ -208,7 +207,7 @@
 
             return carry
 
-        lax.fori_loop(1, count, body, 0)
+        lax.fori_loop(first, last or count, body, 0)
 
     def everything(kind, plane, bulk):
         count, me, where = over(kind)
@@ -316,10 +315,11 @@
     def _():
         left_out.start()
 
-    HAND_GL, HAND_A, HAND_B, HAND_LEFT, HAND_OUT, HAND_SW = 12, 13, 14, 15, 16, 10
+    HAND_GL, HAND_A, HAND_B, HAND_LEFT, HAND_OUT, HAND_SW, HAND_SV = 12, 13, 14, 15, 1, 10, 7
 
     def passed(i, q):
-        row = 2 * lax.rem(r // 2 + i, rows // 2) + core
+        begin = jnp.minimum((r + 1 - core) // 2, rows // 2 - 1)
+        row = 2 * lax.rem(begin + i, rows // 2) + core
         near = (r * factor + q) // 2 == chip
         return row * factor + q, near, jnp.logical_and(row == r, r * factor + q == c)
 
@@ -352,7 +352,7 @@
 
     right_args = ("row", 0, lambda k: right_block(r), right_block, grr_ref)
 
-    start(*right_args)
+    start(*right_args, last=2)
     for k in late:
         loads[k].wait()
     owf_ref[...] = ow_ref[...].astype(F32)
@@ -384,6 +384,7 @@
 
     steps = pairs // WIDE
     lax.fori_loop(0, steps // 2, grad_products, 0)
+    start(*right_args, first=2)
     pass_left(0)
     lax.fori_loop(steps // 2, steps, grad_products, 0)
 
@@ -583,15 +584,18 @@
     grad_w_in = joined[:, :channels]
     low_sum = jnp.sum(low_ref[...].astype(F32), axis=0, keepdims=True)
     turned = w_turned.astype(F32)
-    sv_ref[0:1, :] = jnp.sum(joined[:, channels:] * turned, axis=0, keepdims=True)
-    sv_ref[1:2, :] = jnp.sum(low_sum.T * turned, axis=0, keepdims=True)
+    gain_sum = jnp.sum(joined[:, channels:] * turned, axis=0, keepdims=True)
+    shift_sum = jnp.sum(low_sum.T * turned, axis=0, keepdims=True)
+    parts = channels // LANES
+    sv_ref[...] = jnp.zeros(sv_ref.shape, F32)
+    for k in range(parts):
+        sv_ref[k : k + 1, :] = gain_sum[:, k * LANES : (k + 1) * LANES]
+        sv_ref[parts + k : parts + k + 1, :] = shift_sum[:, k * LANES : (k + 1) * LANES]
+    sv_ref[2 * parts : 2 * parts + 1, :] = bias_sum
     quarter = 2 * hidden // cols
     for k in range(cols):
         sw_ref[k] = grad_w_in[k * quarter : (k + 1) * quarter, :].astype(BF16)
-    sv_ref[2:3, :] = jnp.concatenate([bias_sum, jnp.zeros((1, channels - LANES), F32)], axis=1)
-    sv_ref[3:8, :] = jnp.zeros((5, channels), F32)
-    sv_row_args = ("col", 7, lambda k: sv_ref, lambda k: svr_ref.at[k], svr_ref)
-    start(*sv_row_args)
+    hand(HAND_SV, sv_ref, svp_ref.at[0])
 
     def hand_sw(k, carry):
         hand(HAND_SW, sw_ref.at[2 * k + 1 - core], swp_ref.at[k])
@@ -619,6 +623,10 @@
     lax.fori_loop(0, chips, add_sw, 0)
     sw_args = ("core", 6, lambda k: swx_ref.at[lax.rem(k, chips)], lambda k: swr_ref.at[k], swr_ref)
     start(*sw_args)
+    handed(HAND_SV, svp_ref).wait_recv()
+    svc_ref[...] = sv_ref[...] + svp_ref[0]
+    sv_args = ("core", 8, lambda k: svc_ref, lambda k: svr_ref.at[k], svr_ref)
+    start(*sv_args)
     receive(*gw_col_args)
 
     def add_w_col(t, carry):
@@ -642,29 +650,23 @@
 
         return lax.fori_loop(1, count, add, received[0].astype(F32))
 
-    svr_ref[c] = sv_ref[...]
-    receive(*sv_row_args)
-    svc_ref[...] = ordered(svr_ref, cols)
-    sv_col_args = ("row", 8, lambda k: svc_ref, lambda k: svcr_ref.at[k], svcr_ref)
-    start(*sv_col_args)
-
-    receive(*gw_all_args)
-
-    def hand_out(k, carry):
-        slot = gw_ref.at[2 * k + core]
-        hand(HAND_OUT, slot, slot)
-        return carry
-
-    lax.fori_loop(0, chips, hand_out, 0)
     swr_ref[r * chips + chip] = swx_ref[chip]
     receive(*sw_args)
     swf_ref[...] = ordered(swr_ref, rows * chips)
     gpw_ref[c] = swf_ref[...]
     sw_out_args = ("col", 11, lambda k: swf_ref, lambda k: gpw_ref.at[k], gpw_ref)
     start(*sw_out_args)
-    svcr_ref[r] = svc_ref[...]
-    receive(*sv_col_args)
-    vec_ref[...] = ordered(svcr_ref, rows)
+    receive(*gw_all_args)
+
+    def hand_out(k, carry):
+        slot = gw_ref.at[2 * k + core]
+        hand(HAND_OUT, slot, slot)
+        return carry
+
+    lax.fori_loop(0, chips, hand_out, 0)
+    svr_ref[r * chips + chip] = svc_ref[...]
+    receive(*sv_args)
+    vec_ref[...] = ordered(svr_ref, rows * chips)
     handed(HAND_OUT, gw_ref.at[pl.ds(0, chips)]).wait_recv()
     for t in range(cols):
         for k in range(rows):
@@ -693,6 +695,7 @@
 
     handed(HAND_LEFT, glp_ref).wait_send()
     handed(HAND_SW, swp_ref).wait_send()
+    handed(HAND_SV, svp_ref).wait_send()
     handed(HAND_GL, glp_ref).wait_send()
     handed(HAND_OUT, gw_ref.at[pl.ds(0, chips)]).wait_send()
     for plane in (HAND_A, HAND_B):
@@ -704,34 +707,36 @@
         gw_row_args,
         gw_col_args,
         sw_args,
-        sv_row_args,
+        sv_args,
         gw_all_args,
-        sv_col_args,
         sw_out_args,
     ):
         drain(*args)
 
 
-def finish_kernel(pair_ref, ag_ref, gw_ref, gpw_ref, vec_ref, pair_hbm, ag_hbm, gain_ref, shift_ref, gpw_out, bias_ref, gw_hbm, sems):
+def finish_kernel(*refs):
+    pair_ref, ag_ref, gw_ref, gpw_ref, vec_ref = refs[:5]
+    pair_hbm, ag_hbm, gain_hbm, shift_hbm, gpw_hbm, bias_hbm, gw_hbm = refs[5:12]
+    gain_ref, shift_ref, bias_ref, sems = refs[12:]
     copies = []
 
-    def send(source, target, parts, part):
-        size = source.shape[0] // parts
-        here = pl.ds(part * size, size)
-        copy = pltpu.make_async_copy(source.at[here, :], target.at[here, :], sems.at[len(copies)])
+    def send(source, target):
+        copy = pltpu.make_async_copy(source, target, sems.at[len(copies)])
         copy.start()
         copies.append(copy)
 
-    for part in range(4):
-        send(ag_ref, ag_hbm, 4, part)
-    for part in range(2):
-        send(pair_ref, pair_hbm, 2, part)
-    for part in range(4):
-        send(gw_ref, gw_hbm, 4, part)
-    gain_ref[...] = vec_ref[0:1, :]
-    shift_ref[...] = vec_ref[1:2, :]
-    bias_ref[...] = vec_ref[2:3, : bias_ref.shape[1]]
-    gpw_out[...] = gpw_ref[...]
+    send(gw_ref, gw_hbm)
+    send(ag_ref, ag_hbm)
+    send(pair_ref, pair_hbm)
+    send(gpw_ref, gpw_hbm)
+    parts = gain_ref.shape[1] // LANES
+    for k in range(parts):
+        gain_ref[:, k * LANES : (k + 1) * LANES] = vec_ref[k : k + 1, :]
+        shift_ref[:, k * LANES : (k + 1) * LANES] = vec_ref[parts + k : parts + k + 1, :]
+    bias_ref[...] = vec_ref[2 * parts : 2 * parts + 1, : bias_ref.shape[1]]
+    send(gain_ref, gain_hbm)
+    send(shift_ref, shift_hbm)
+    send(bias_ref, bias_hbm)
     for copy in copies:
         copy.wait()
 
@@ -787,7 +792,7 @@
             jax.ShapeDtypeStruct((n, channels), BF16),
             jax.ShapeDtypeStruct((hidden * hidden, width), F32),
             jax.ShapeDtypeStruct((cols, quarter, channels), F32),
-            jax.ShapeDtypeStruct((8, channels), F32),
+            jax.ShapeDtypeStruct((8, LANES), F32),
         ],
         in_specs=[hbm] * 10,
         out_specs=[vmem] * 5,
@@ -831,14 +836,14 @@
             pltpu.VMEM((cols // 2, quarter, channels), BF16),
             pltpu.VMEM((rows * cols // 2, quarter, channels), BF16),
             pltpu.VMEM((quarter, channels), F32),
-            pltpu.VMEM((8, channels), F32),
-            pltpu.VMEM((cols, 8, channels), F32),
-            pltpu.VMEM((8, channels), F32),
-            pltpu.VMEM((rows, 8, channels), F32),
+            pltpu.VMEM((8, LANES), F32),
+            pltpu.VMEM((rows * cols // 2, 8, LANES), F32),
+            pltpu.VMEM((1, 8, LANES), F32),
+            pltpu.VMEM((8, LANES), F32),
             pltpu.SemaphoreType.DMA((12,)),
             pltpu.SemaphoreType.DMA((4,)),
-            pltpu.SemaphoreType.DMA((17,)),
-            pltpu.SemaphoreType.DMA((17,)),
+            pltpu.SemaphoreType.DMA((16,)),
+            pltpu.SemaphoreType.DMA((16,)),
             pltpu.SemaphoreType.DMA((cols,)),
             pltpu.SemaphoreType.DMA((cols,)),
         ],
@@ -858,9 +863,12 @@
             jax.ShapeDtypeStruct((hidden * hidden, width), F32),
         ],
         in_specs=[vmem] * 5,
-        out_specs=[hbm, hbm, vmem, vmem, vmem, vmem, hbm],
+        out_specs=[hbm] * 7,
         scratch_shapes=[
-            pltpu.SemaphoreType.DMA((10,)),
+            pltpu.VMEM((1, channels), F32),
+            pltpu.VMEM((1, channels), F32),
+            pltpu.VMEM((1, 2 * hidden), F32),
+            pltpu.SemaphoreType.DMA((7,)),
         ],
         compiler_params=pltpu.CompilerParams(vmem_limit_bytes=16 * 1024 * 1024),
     )(pair, grad_alignment, grad_w, grad_pw.reshape(-1, channels), vectors)

time: 39 us -> 36.8 us (0.944)
  Pallas kernels: 38.2 us -> 36 us
    pallas_call x1, Pallas kernels: 36.4 us -> 34.8 us  [shards(): pl.pallas_call(functools.partial(fused_kernel, dims), out_shape=[jax.Shap...]
    pallas_call x1, Pallas kernels: 1.77 us -> 1.13 us  [shards(): pl.pallas_call(finish_kernel, out_shape=[jax.ShapeDtypeStruct((pairs, wid...]
where the time goes in v4:
time: 36.8 us; the launch traced here: 36.6 us
  Pallas kernels  36 us (98%)
  between operations  0.64 us (2%)
    pallas_call x1, Pallas kernels, shards(): pl.pallas_call(functools.partial(fused_kernel, dims), out_shape=[jax.Shap...  34.8 us
    pallas_call x1, Pallas kernels, shards(): pl.pallas_call(finish_kernel, out_shape=[jax.ShapeDtypeStruct((pairs, wid...  1.13 us

profile of v4, /device:TPU:0, one launch (start us, length us, event | category | flops | bytes accessed | tf_op | source)
XLA Modules:
  0.0 36.6 jit_solution(11309909243483887779)
XLA Ops:
  0.6 34.8 %shard_map.153 = (bf16[1024,128]{1,0:T(8,128)(2,1)S(1)}, bf16[1024,256]{1,0:T(8,128)(2,1)S(1)}, f32[1024,128]{1,0:T(8,128)S(1)}, f32[4,16,256]{2,1,0:T(8,128)S(1)}, f32[8,128]{1,0:T(8,128)S(1)}) custom-call(bf16[1024,256]{1,0:T(8,128)(2,1)} %bitcast.17, s32[1,128]{1,0:T(1,128)} %bitcast.22, s32[1,128]{1,0:T(1,128)} %bitcast.23, f32[1,256]{1,0:T(1,128)} %bitcast.20, ...), custom_call_target="tpu_custom_call" | custom-call | tf_op jit(solution)/shard_map/pallas_call | solution.py:788
  35.5 1.1 %shard_map.154 = (bf16[1024,128]{1,0:T(8,128)(2,1)}, bf16[1024,256]{1,0:T(8,128)(2,1)}, f32[1,256]{1,0:T(1,128)}, f32[1,256]{1,0:T(1,128)}, f32[64,256]{1,0:T(8,...) custom-call(bf16[1024,128]{1,0:T(8,128)(2,1)S(1)} %get-tuple-element.19.refs_0_, ...), custom_call_target="tpu_custom_call" | custom-call | tf_op jit(solution)/shard_map/pallas_call | solution.py:854

commit v5 on v4

--- a/solution.py
+++ b/solution.py
@@ -413,8 +413,11 @@
     for k in range(tile_rows * hidden // WIDE):
         gls_ref[:, k * WIDE : (k + 1) * WIDE] = nt(rbuf_ref[...], gp_ref[k * WIDE : (k + 1) * WIDE, :]).astype(BF16)
 
+    def left_block(k, of_core):
+        return of_core * chips + k
+
     def hand_left(k, carry):
-        hand(HAND_GL, gl_part((1 - core) * chips + k), glp_ref.at[k])
+        hand(HAND_GL, gl_part(left_block(k, 1 - core)), glp_ref.at[k])
         return carry
 
     lax.fori_loop(0, chips, hand_left, 0)
@@ -424,7 +427,7 @@
         handed(HAND_GL, glp_ref).wait_recv()
 
         def add(k, carry):
-            t = core * chips + k
+            t = left_block(k, core)
             mine = gls_ref[aligned((t // factor) * seq_local, seq_local), aligned(lax.rem(t, factor) * block, block)]
             glx_ref[k] = (mine.astype(F32) + glp_ref[k].astype(F32)).astype(BF16)
             return carry
@@ -499,7 +502,7 @@
         return carry + glr_ref[lax.rem(chip + t, chips)].astype(F32)
 
     glmid_ref[...] = lax.fori_loop(1, chips, add_left, glx_ref[chip].astype(F32)).astype(BF16)
-    gathered = core * chips + chip
+    gathered = left_block(chip, core)
     owner_row = gathered // factor
     owner_col = r * factor + lax.rem(gathered, factor)
     at_home = jnp.logical_and(owner_row == r, owner_col == c)
@@ -551,6 +554,15 @@
             turned = place_groups(pieces, [(q - k) * res_local for q in range(fold)], res_local)
             tr_ref[pl.ds(sb * LANES + hidden + k, majors, stride=fold), :] = turned
 
+    lane = lax.broadcasted_iota(jnp.int32, (LANES, LANES), 1)
+
+    def lower_right(k, carry):
+        here = aligned(k * LANES, LANES)
+        right_only = jnp.logical_and(lane >= hidden, lane < 2 * hidden)
+        tr_ref[here, :] = jnp.where(right_only, tr_ref[here, :].T * live_column(k), 0.0)
+        return carry
+
+    lax.fori_loop(0, chunks, lower_right, 0, unroll=min(2 * UNROLL, chunks))
     giver = r * factor + lax.rem(c, factor)
     giver_row = c // factor
     giver_col = 2 * lax.rem(giver, chips) + giver // chips
@@ -570,12 +582,9 @@
             rolled = pltpu.roll(piece, LANES - k * hidden, 1) if k else piece
             prj_ref[pl.ds(im * fold + k, seq_local, stride=res_local), :] = rolled
 
-    lane = lax.broadcasted_iota(jnp.int32, (LANES, LANES), 1)
-
     def lower(k, bias_sum):
         here = aligned(k * LANES, LANES)
-        projected = jnp.where(lane < hidden, prj_ref[here, :], tr_ref[here, :].T)
-        projected = jnp.where(lane < 2 * hidden, projected * live_column(k), 0.0)
+        projected = jnp.where(lane < hidden, prj_ref[here, :] * live_column(k), tr_ref[here, :])
         low_ref[here, :] = projected.astype(BF16)
         return bias_sum + jnp.sum(projected, axis=0, keepdims=True)
 
@@ -667,11 +676,18 @@
     svr_ref[r * chips + chip] = svc_ref[...]
     receive(*sv_args)
     vec_ref[...] = ordered(svr_ref, rows * chips)
+    def widen(of_core):
+        def body(t, carry):
+            for k in range(rows):
+                at = (2 * t + of_core) * rows * w_small + k * w_small
+                owf_ref[aligned(at, w_small), :] = gw_ref[2 * t + of_core, k].astype(F32)
+            return carry
+
+        lax.fori_loop(0, chips, body, 0)
+
+    widen(core)
     handed(HAND_OUT, gw_ref.at[pl.ds(0, chips)]).wait_recv()
-    for t in range(cols):
-        for k in range(rows):
-            at = (t * rows + k) * w_small
-            owf_ref[at : at + w_small, :] = gw_ref[t, k].astype(F32)
+    widen(1 - core)
     for k in range(hidden):
         gwf_ref[k * hidden : (k + 1) * hidden, :] = owf_ref[pl.ds(k, hidden, stride=hidden), :]
     receive(*sw_out_args)

time: 36.8 us -> 36.8 us (level)
  no operation moved by 1% of the time
where the time goes in v5:
time: 36.8 us; the launch traced here: 36.6 us
  Pallas kernels  36 us (98%)
  between operations  0.64 us (2%)
    pallas_call x1, Pallas kernels, shards(): pl.pallas_call(functools.partial(fused_kernel, dims), out_shape=[jax.Shap...  34.9 us
    pallas_call x1, Pallas kernels, shards(): pl.pallas_call(finish_kernel, out_shape=[jax.ShapeDtypeStruct((pairs, wid...  1.13 us

profile of v5, /device:TPU:0, one launch (start us, length us, event | category | flops | bytes accessed | tf_op | source)
XLA Modules:
  0.0 36.6 jit_solution(2148470171638325611)
XLA Ops:
  0.6 34.9 %shard_map.153 = (bf16[1024,128]{1,0:T(8,128)(2,1)S(1)}, bf16[1024,256]{1,0:T(8,128)(2,1)S(1)}, f32[1024,128]{1,0:T(8,128)S(1)}, f32[4,16,256]{2,1,0:T(8,128)S(1)}, f32[8,128]{1,0:T(8,128)S(1)}) custom-call(bf16[1024,256]{1,0:T(8,128)(2,1)} %bitcast.17, s32[1,128]{1,0:T(1,128)} %bitcast.22, s32[1,128]{1,0:T(1,128)} %bitcast.23, f32[1,256]{1,0:T(1,128)} %bitcast.20, ...), custom_call_target="tpu_custom_call" | custom-call | tf_op jit(solution)/shard_map/pallas_call | solution.py:804
  35.5 1.1 %shard_map.154 = (bf16[1024,128]{1,0:T(8,128)(2,1)}, bf16[1024,256]{1,0:T(8,128)(2,1)}, f32[1,256]{1,0:T(1,128)}, f32[1,256]{1,0:T(1,128)}, f32[64,256]{1,0:T(8,...) custom-call(bf16[1024,128]{1,0:T(8,128)(2,1)S(1)} %get-tuple-element.19.refs_0_, ...), custom_call_target="tpu_custom_call" | custom-call | tf_op jit(solution)/shard_map/pallas_call | solution.py:870

commit v6 on v5

--- a/solution.py
+++ b/solution.py
@@ -315,7 +315,7 @@
     def _():
         left_out.start()
 
-    HAND_GL, HAND_A, HAND_B, HAND_LEFT, HAND_OUT, HAND_SW, HAND_SV = 12, 13, 14, 15, 1, 10, 7
+    HAND_GL, HAND_A, HAND_B, HAND_LEFT, HAND_OUT, HAND_SW, HAND_SV, HAND_SWR = 12, 13, 14, 15, 1, 10, 7, 16
 
     def passed(i, q):
         begin = jnp.minimum((r + 1 - core) // 2, rows // 2 - 1)
@@ -559,10 +559,49 @@
     def lower_right(k, carry):
         here = aligned(k * LANES, LANES)
         right_only = jnp.logical_and(lane >= hidden, lane < 2 * hidden)
-        tr_ref[here, :] = jnp.where(right_only, tr_ref[here, :].T * live_column(k), 0.0)
+        right_part = jnp.where(right_only, tr_ref[here, :].T * live_column(k), 0.0)
+        tr_ref[here, :] = right_part
+        low_ref[here, :] = right_part.astype(BF16)
         return carry
 
     lax.fori_loop(0, chunks, lower_right, 0, unroll=min(2 * UNROLL, chunks))
+    quarter = 2 * hidden // cols
+    sw_args = ("core", 6, lambda k: swx_ref.at[lax.rem(k, chips)], lambda k: swr_ref.at[k], swr_ref)
+    few = chips // 2
+
+    def hand_quarters(plane, low_chip, summed_over):
+        for k in range(2 * low_chip, 2 * (low_chip + few)):
+            sw_ref[k] = summed_over[k * quarter : (k + 1) * quarter, :].astype(BF16)
+
+        def body(k, carry):
+            hand(plane, sw_ref.at[2 * k + 1 - core], swp_ref.at[k])
+            return carry
+
+        lax.fori_loop(low_chip, low_chip + few, body, 0)
+
+    def send_quarters(plane, low_chip):
+        handed(plane, swp_ref.at[pl.ds(low_chip, few)]).wait_recv()
+
+        def add(k, carry):
+            swx_ref[k] = (sw_ref[2 * k + core].astype(F32) + swp_ref[k].astype(F32)).astype(BF16)
+            return carry
+
+        lax.fori_loop(low_chip, low_chip + few, add, 0)
+
+        def body(t, carry):
+            k = lax.rem(r * chips + chip + t, rows * chips)
+            target = lax.rem(k, chips)
+
+            @pl.when(jnp.logical_and(target >= low_chip, target < low_chip + few))
+            def _():
+                send_to(sw_args, k)
+
+            return carry
+
+        lax.fori_loop(1, rows * chips, body, 0)
+
+    hand_quarters(HAND_SWR, few, tn(low_ref[...], both_ref[:, :channels]))
+    send_quarters(HAND_SWR, few)
     giver = r * factor + lax.rem(c, factor)
     giver_row = c // factor
     giver_col = 2 * lax.rem(giver, chips) + giver // chips
@@ -601,17 +640,9 @@
         sv_ref[k : k + 1, :] = gain_sum[:, k * LANES : (k + 1) * LANES]
         sv_ref[parts + k : parts + k + 1, :] = shift_sum[:, k * LANES : (k + 1) * LANES]
     sv_ref[2 * parts : 2 * parts + 1, :] = bias_sum
-    quarter = 2 * hidden // cols
-    for k in range(cols):
-        sw_ref[k] = grad_w_in[k * quarter : (k + 1) * quarter, :].astype(BF16)
     hand(HAND_SV, sv_ref, svp_ref.at[0])
 
-    def hand_sw(k, carry):
-        hand(HAND_SW, sw_ref.at[2 * k + 1 - core], swp_ref.at[k])
-        return carry
-
-    lax.fori_loop(0, chips, hand_sw, 0)
-
+    hand_quarters(HAND_SW, 0, grad_w_in)
     def backward(k, carry):
         here = aligned(k * LANES, LANES)
         scaled = scaled_ref[here, :]
@@ -623,15 +654,7 @@
 
     split = chunks // 2
     lax.fori_loop(0, split, backward, 0, unroll=min(UNROLL, split))
-    handed(HAND_SW, swp_ref).wait_recv()
-
-    def add_sw(k, carry):
-        swx_ref[k] = (sw_ref[2 * k + core].astype(F32) + swp_ref[k].astype(F32)).astype(BF16)
-        return carry
-
-    lax.fori_loop(0, chips, add_sw, 0)
-    sw_args = ("core", 6, lambda k: swx_ref.at[lax.rem(k, chips)], lambda k: swr_ref.at[k], swr_ref)
-    start(*sw_args)
+    send_quarters(HAND_SW, 0)
     handed(HAND_SV, svp_ref).wait_recv()
     svc_ref[...] = sv_ref[...] + svp_ref[0]
     sv_args = ("core", 8, lambda k: svc_ref, lambda k: svr_ref.at[k], svr_ref)
@@ -710,7 +733,8 @@
                 remote(rest, rest, left_send.at[k], left_recv.at[k], r, partner).wait_send()
 
     handed(HAND_LEFT, glp_ref).wait_send()
-    handed(HAND_SW, swp_ref).wait_send()
+    for plane in (HAND_SW, HAND_SWR):
+        handed(plane, swp_ref.at[pl.ds(0, few)]).wait_send()
     handed(HAND_SV, svp_ref).wait_send()
     handed(HAND_GL, glp_ref).wait_send()
     handed(HAND_OUT, gw_ref.at[pl.ds(0, chips)]).wait_send()
@@ -858,8 +882,8 @@
             pltpu.VMEM((8, LANES), F32),
             pltpu.SemaphoreType.DMA((12,)),
             pltpu.SemaphoreType.DMA((4,)),
-            pltpu.SemaphoreType.DMA((16,)),
-            pltpu.SemaphoreType.DMA((16,)),
+            pltpu.SemaphoreType.DMA((17,)),
+            pltpu.SemaphoreType.DMA((17,)),
             pltpu.SemaphoreType.DMA((cols,)),
             pltpu.SemaphoreType.DMA((cols,)),
         ],

time: 36.8 us -> 36.1 us (0.981)
  Pallas kernels: 36 us -> 35.1 us
    pallas_call x1, Pallas kernels: 34.9 us -> 34 us  [shards(): pl.pallas_call(functools.partial(fused_kernel, dims), out_shape=[jax.Shap...]
where the time goes in v6:
time: 36.1 us; the launch traced here: 35.8 us
  Pallas kernels  35.1 us (97%)
  between operations  0.64 us (2%)
    pallas_call x1, Pallas kernels, shards(): pl.pallas_call(functools.partial(fused_kernel, dims), out_shape=[jax.Shap...  34 us
    pallas_call x1, Pallas kernels, shards(): pl.pallas_call(finish_kernel, out_shape=[jax.ShapeDtypeStruct((pairs, wid...  1.13 us

profile of v6, /device:TPU:0, one launch (start us, length us, event | category | flops | bytes accessed | tf_op | source)
XLA Modules:
  0.0 35.8 jit_solution(18327725419224452992)
XLA Ops:
  0.6 34.0 %shard_map.153 = (bf16[1024,128]{1,0:T(8,128)(2,1)S(1)}, bf16[1024,256]{1,0:T(8,128)(2,1)S(1)}, f32[1024,128]{1,0:T(8,128)S(1)}, f32[4,16,256]{2,1,0:T(8,128)S(1)}, f32[8,128]{1,0:T(8,128)S(1)}) custom-call(bf16[1024,256]{1,0:T(8,128)(2,1)} %bitcast.17, s32[1,128]{1,0:T(1,128)} %bitcast.22, s32[1,128]{1,0:T(1,128)} %bitcast.23, f32[1,256]{1,0:T(1,128)} %bitcast.20, ...), custom_call_target="tpu_custom_call" | custom-call | tf_op jit(solution)/shard_map/pallas_call | solution.py:828
  34.7 1.1 %shard_map.154 = (bf16[1024,128]{1,0:T(8,128)(2,1)}, bf16[1024,256]{1,0:T(8,128)(2,1)}, f32[1,256]{1,0:T(1,128)}, f32[1,256]{1,0:T(1,128)}, f32[64,256]{1,0:T(8,...) custom-call(bf16[1024,128]{1,0:T(8,128)(2,1)S(1)} %get-tuple-element.19.refs_0_, ...), custom_call_target="tpu_custom_call" | custom-call | tf_op jit(solution)/shard_map/pallas_call | solution.py:894

commit v7 on v6

--- a/solution.py
+++ b/solution.py
@@ -601,7 +601,6 @@
         lax.fori_loop(1, rows * chips, body, 0)
 
     hand_quarters(HAND_SWR, few, tn(low_ref[...], both_ref[:, :channels]))
-    send_quarters(HAND_SWR, few)
     giver = r * factor + lax.rem(c, factor)
     giver_row = c // factor
     giver_col = 2 * lax.rem(giver, chips) + giver // chips
@@ -621,6 +620,7 @@
             rolled = pltpu.roll(piece, LANES - k * hidden, 1) if k else piece
             prj_ref[pl.ds(im * fold + k, seq_local, stride=res_local), :] = rolled
 
+    send_quarters(HAND_SWR, few)
     def lower(k, bias_sum):
         here = aligned(k * LANES, LANES)
         projected = jnp.where(lane < hidden, prj_ref[here, :] * live_column(k), tr_ref[here, :])

time: 36.1 us -> 35.9 us (level)
  no operation moved by 1% of the time
where the time goes in v7:
time: 35.9 us; the launch traced here: 35.8 us
  Pallas kernels  35.1 us (98%)
  between operations  0.64 us (2%)
    pallas_call x1, Pallas kernels, shards(): pl.pallas_call(functools.partial(fused_kernel, dims), out_shape=[jax.Shap...  34 us
    pallas_call x1, Pallas kernels, shards(): pl.pallas_call(finish_kernel, out_shape=[jax.ShapeDtypeStruct((pairs, wid...  1.13 us

profile of v7, /device:TPU:0, one launch (start us, length us, event | category | flops | bytes accessed | tf_op | source)
XLA Modules:
  0.0 35.8 jit_solution(10758135132730874151)
XLA Ops:
  0.6 34.0 %shard_map.153 = (bf16[1024,128]{1,0:T(8,128)(2,1)S(1)}, bf16[1024,256]{1,0:T(8,128)(2,1)S(1)}, f32[1024,128]{1,0:T(8,128)S(1)}, f32[4,16,256]{2,1,0:T(8,128)S(1)}, f32[8,128]{1,0:T(8,128)S(1)}) custom-call(bf16[1024,256]{1,0:T(8,128)(2,1)} %bitcast.17, s32[1,128]{1,0:T(1,128)} %bitcast.22, s32[1,128]{1,0:T(1,128)} %bitcast.23, f32[1,256]{1,0:T(1,128)} %bitcast.20, ...), custom_call_target="tpu_custom_call" | custom-call | tf_op jit(solution)/shard_map/pallas_call | solution.py:828
  34.6 1.1 %shard_map.154 = (bf16[1024,128]{1,0:T(8,128)(2,1)}, bf16[1024,256]{1,0:T(8,128)(2,1)}, f32[1,256]{1,0:T(1,128)}, f32[1,256]{1,0:T(1,128)}, f32[64,256]{1,0:T(8,...) custom-call(bf16[1024,128]{1,0:T(8,128)(2,1)S(1)} %get-tuple-element.19.refs_0_, ...), custom_call_target="tpu_custom_call" | custom-call | tf_op jit(solution)/shard_map/pallas_call | solution.py:894
